TPU v7x, 32 devices: a whole 2x2x4 slice. The times are simulated.
32 devices in a mesh: rep: 4 (over z), shard: 8 (over y, x, core).
Axes of the slice: x: 2, y: 2, z: 4, core: 2. Of those that a mesh axis runs over, the one named last changes fastest.
Arguments:
- tokens: bfloat16 [8192, 1024], P(('rep', 'shard')), may hold values from -6 to 6
- prefix: int32 [32], P(('rep', 'shard')), may hold values from 25 to 128
- routes: int32 [8192, 8], P(('rep', 'shard')), may hold values from 0 to 31, all different within a row; in each aligned block of 256 rows (0 to 255, 256 to 511, ...) at most 96 rows name the same one
- cotangent: bfloat16 [8192, 1024], P(('rep', 'shard')), may hold values from -6 to 6
- w_query: bfloat16 [1024, 1024], P('shard'), may hold values from -0.625 to 0.625
- key_weight: bfloat16 [1024, 512], P('shard'), may hold values from -0.625 to 0.625
- value_weight: bfloat16 [1024, 512], P('shard'), may hold values from -0.1875 to 0.1875
- w_out: bfloat16 [1024, 1024], P('shard'), may hold values from -6 to 6
- norm_attn: bfloat16 [1024], P('shard'), may hold values from 0.5 to 1.5
- norm_moe: bfloat16 [1024], P('shard'), may hold values from 0.5 to 1.5
- w_router: bfloat16 [1024, 32], P('shard'), may hold values from -0.09375 to 0.09375
- w_gate: bfloat16 [32, 1024, 512], P('shard'), may hold values from -0.1875 to 0.1875
- w_up: bfloat16 [32, 1024, 512], P('shard'), may hold values from -0.1875 to 0.1875
- w_down: bfloat16 [32, 512, 1024], P('shard'), may hold values from -6 to 6
Outputs:
- layer_out: bfloat16 [8192, 1024], P(('rep', 'shard'))
- d_tokens: float32 [8192, 1024], P(('rep', 'shard'))
- d_w_query: float32 [1024, 1024], P('shard')
- d_w_key: float32 [1024, 512], P('shard')
- d_w_value: float32 [1024, 512], P('shard')
- d_w_out: float32 [1024, 1024], P('shard')
- d_norm_attn: float32 [1024], P('shard')
- d_norm_moe: float32 [1024], P('shard')
- d_w_router: float32 [1024, 32], P('shard')
- d_w_gate: float32 [32, 1024, 512], P('shard')
- d_w_up: float32 [32, 1024, 512], P('shard')
- d_w_down: float32 [32, 512, 1024], P('shard')
Inputs may be any that keep to these rules, and one draw needn't show every extreme that they name: `routes`: each row names 8 different experts; among the rows of one device no expert is named more than 96 times, and in every draw some device's rows name some expert exactly 96 times.
All inputs are finite; a program needn't handle non-finite values.
Results may differ from a plain program's by a relative error of at most 0.024.
Values may be sent and summed in bfloat16 or wider, within the bound.
A program may use at most 256 MiB of HBM per device.

v0:
```python
import math

import jax
import jax.numpy as jnp
from jax import lax
from jax.sharding import PartitionSpec as P

MODEL_WIDTH = 1024
QUERY_HEADS = 16
KEY_VALUE_HEADS = 8
HEAD_SIZE = 64
EXPERTS = 32
TOP = 8
CAP = 96


epsilon = 1e-06
score_scale = 0.015625
branch_scale = 0.22
masked_value = -1e30


def norm_scale(value_rows):
    return lax.rsqrt(jnp.mean(value_rows * value_rows, axis=-1, keepdims=True) + epsilon)


def norm_backward(value_rows, scaling, norm_gain, upstream):
    weighted = upstream * norm_gain
    inner_mean = jnp.mean(weighted * value_rows, axis=-1, keepdims=True)
    value_gradient = scaling * weighted - value_rows * (scaling * scaling * scaling) * inner_mean
    d_gain = jnp.sum(upstream * value_rows * scaling, axis=0)
    return (value_gradient, d_gain)


def rotary_tables(positions_count):
    half_size = HEAD_SIZE // 2
    places = jnp.arange(positions_count, dtype=jnp.float32)
    inverse = jnp.exp(
        jnp.arange(half_size, dtype=jnp.float32) * (-2.0 * math.log(10000.0) / HEAD_SIZE)
    )
    angles = places[:, None] * inverse[None, :]
    return (jnp.cos(angles)[:, None, :], jnp.sin(angles)[:, None, :])


def apply_rotary(value_rows, cosine_table, sine_table):
    half_size = value_rows.shape[-1] // 2
    first_half = value_rows[..., :half_size]
    second_half = value_rows[..., half_size:]
    return jnp.concatenate(
        [
            first_half * cosine_table - second_half * sine_table,
            second_half * cosine_table + first_half * sine_table,
        ],
        axis=-1,
    )


def outer_sum(left_rows, right_rows):
    return lax.dot_general(
        left_rows, right_rows, (((0,), (0,)), ((), ())), preferred_element_type=jnp.float32
    )


def back_product(grad_rows, weight_rows):
    return lax.dot_general(
        grad_rows, weight_rows, (((1,), (1,)), ((), ())), preferred_element_type=jnp.float32
    )


def slot_places(route_rows):
    flat_routes = route_rows.reshape(-1)
    expert_ids = jnp.arange(EXPERTS, dtype=jnp.int32)
    matches = (flat_routes[:, None] == expert_ids[None, :]).astype(jnp.int32)
    earlier = jnp.cumsum(matches, axis=0) - matches
    return flat_routes * CAP + jnp.sum(earlier * matches, axis=1)


def split_rows(tensor_rows):
    count_of_rows = tensor_rows.shape[0]
    block_rows = min(512, count_of_rows)
    shaped = tensor_rows.reshape((count_of_rows // block_rows, block_rows) + tensor_rows.shape[1:])
    return (shaped, jnp.arange(count_of_rows // block_rows, dtype=jnp.int32) * block_rows)


def masked_scores(query_rows, key_rows, first_row, prefix_len):
    block_rows = query_rows.shape[0]
    raw_scores = jnp.einsum(
        "tngd,snd->ngts", query_rows, key_rows, preferred_element_type=jnp.float32
    )
    row_index = first_row + jnp.arange(block_rows, dtype=jnp.int32)
    key_index = jnp.arange(key_rows.shape[0], dtype=jnp.int32)
    visible = (key_index[None, :] <= row_index[:, None]) | (key_index[None, :] < prefix_len)
    return jnp.where(visible, raw_scores * score_scale, masked_value)


def attention_forward(query_matrix, key_rows, value_rows, prefix_len):
    query_blocks, first_rows = split_rows(query_matrix)

    def one_block(arguments):
        query_rows, first_row = arguments
        scores = masked_scores(query_rows, key_rows, first_row, prefix_len)
        highest_precision = jnp.max(scores, axis=-1, keepdims=True)
        weights = jnp.exp(scores - highest_precision)
        totals = jnp.sum(weights, axis=-1, keepdims=True)
        probabilities = (weights / totals).astype(jnp.bfloat16)
        attended = jnp.einsum(
            "ngts,snd->tngd", probabilities, value_rows, preferred_element_type=jnp.float32
        )
        return (attended, highest_precision + jnp.log(totals))

    attended, log_sums = lax.map(one_block, (query_blocks, first_rows))
    return (attended.reshape(query_matrix.shape), log_sums)


def attention_backward(query_matrix, key_rows, value_rows, d_attended, log_sums, prefix_len):
    query_blocks, first_rows = split_rows(query_matrix)
    grad_blocks, unused_rows = split_rows(d_attended)

    def one_block(carried, arguments):
        key_gradient, value_gradient = carried
        query_rows, grad_rows, sum_rows, first_row = arguments
        scores = masked_scores(query_rows, key_rows, first_row, prefix_len)
        probabilities = jnp.exp(scores - sum_rows)
        value_gradient = value_gradient + jnp.einsum(
            "ngts,tngd->snd",
            probabilities.astype(jnp.bfloat16),
            grad_rows,
            preferred_element_type=jnp.float32,
        )
        d_probs = jnp.einsum(
            "tngd,snd->ngts", grad_rows, value_rows, preferred_element_type=jnp.float32
        )
        weighted = jnp.sum(probabilities * d_probs, axis=-1, keepdims=True)
        d_scores = (probabilities * (d_probs - weighted) * score_scale).astype(jnp.bfloat16)
        d_query_rows = jnp.einsum(
            "ngts,snd->tngd", d_scores, key_rows, preferred_element_type=jnp.float32
        )
        key_gradient = key_gradient + jnp.einsum(
            "ngts,tngd->snd", d_scores, query_rows, preferred_element_type=jnp.float32
        )
        return ((key_gradient, value_gradient), d_query_rows)

    zeros_kv = jnp.zeros(key_rows.shape, jnp.float32)
    (key_gradient, value_gradient), d_query = lax.scan(
        one_block, (zeros_kv, zeros_kv), (query_blocks, grad_blocks, log_sums, first_rows)
    )
    return (d_query.reshape(query_matrix.shape), key_gradient, value_gradient)


def token_front(layer_weights, inputs, prefix_len, routes):
    w_query, key_weight, value_weight, w_out, norm_attn, norm_moe, w_router = layer_weights
    count_of_rows = inputs.shape[0]
    group_width = QUERY_HEADS // KEY_VALUE_HEADS
    scale_one = norm_scale(inputs)
    first_normed = (inputs * scale_one * norm_attn.astype(jnp.float32)).astype(jnp.bfloat16)
    cosine_table, sine_table = rotary_tables(count_of_rows)
    query_matrix = jnp.dot(first_normed, w_query, preferred_element_type=jnp.float32).reshape(
        count_of_rows, QUERY_HEADS, HEAD_SIZE
    )
    query_matrix = (
        apply_rotary(query_matrix, cosine_table, sine_table)
        .reshape(count_of_rows, KEY_VALUE_HEADS, group_width, HEAD_SIZE)
        .astype(jnp.bfloat16)
    )
    key_rows = jnp.dot(first_normed, key_weight, preferred_element_type=jnp.float32).reshape(
        count_of_rows, KEY_VALUE_HEADS, HEAD_SIZE
    )
    key_rows = apply_rotary(key_rows, cosine_table, sine_table).astype(jnp.bfloat16)
    value_rows = (
        jnp.dot(first_normed, value_weight, preferred_element_type=jnp.float32)
        .reshape(count_of_rows, KEY_VALUE_HEADS, HEAD_SIZE)
        .astype(jnp.bfloat16)
    )
    attended, log_sums = attention_forward(query_matrix, key_rows, value_rows, prefix_len)
    attended = attended.reshape(count_of_rows, QUERY_HEADS * HEAD_SIZE).astype(jnp.bfloat16)
    hidden_one = inputs + branch_scale * jnp.dot(
        attended, w_out, preferred_element_type=jnp.float32
    )
    scale_two = norm_scale(hidden_one)
    normed_two = (hidden_one * scale_two * norm_moe.astype(jnp.float32)).astype(jnp.bfloat16)
    logits = jnp.dot(normed_two, w_router, preferred_element_type=jnp.float32)
    route_picks = (
        routes[:, :, None] == jnp.arange(EXPERTS, dtype=jnp.int32)[None, None, :]
    ).astype(jnp.float32)
    chosen = jnp.sum(route_picks * logits[:, None, :], axis=2)
    route_gates = jax.nn.softmax(chosen, axis=-1)
    places = slot_places(routes)
    dispatched = (
        jnp.zeros((EXPERTS * CAP, MODEL_WIDTH), jnp.bfloat16)
        .at[places]
        .set(jnp.repeat(normed_two, TOP, axis=0))
    )
    dispatched = dispatched.reshape(EXPERTS, CAP, MODEL_WIDTH)
    return (
        scale_one,
        first_normed,
        cosine_table,
        sine_table,
        query_matrix,
        key_rows,
        value_rows,
        log_sums,
        attended,
        hidden_one,
        scale_two,
        normed_two,
        route_picks,
        route_gates,
        places,
        dispatched,
    )


def expert_forward(expert_rows, w_gate, w_up, w_down):
    local_count = w_gate.shape[0]
    four_shape = (
        expert_rows.shape[0] // local_count,
        local_count,
        expert_rows.shape[1],
        expert_rows.shape[2],
    )
    shaped_rows = expert_rows.reshape(four_shape)
    gate_part = jnp.einsum(
        "nlsd,ldf->nlsf", shaped_rows, w_gate, preferred_element_type=jnp.float32
    )
    up_part = jnp.einsum("nlsd,ldf->nlsf", shaped_rows, w_up, preferred_element_type=jnp.float32)
    inner = (jax.nn.silu(gate_part) * up_part).astype(jnp.bfloat16)
    output = jnp.einsum("nlsf,lfd->nlsd", inner, w_down, preferred_element_type=jnp.float32)
    return (gate_part, up_part, output.astype(jnp.bfloat16).reshape(expert_rows.shape))


def expert_backward(expert_rows, expert_grads, gate_part, up_part, w_gate, w_up, w_down):
    local_count = w_gate.shape[0]
    four_shape = (
        expert_rows.shape[0] // local_count,
        local_count,
        expert_rows.shape[1],
        expert_rows.shape[2],
    )
    shaped_rows = expert_rows.reshape(four_shape)
    shaped_grads = expert_grads.reshape(four_shape)
    sigmoid = jax.nn.sigmoid(gate_part)
    activated = jax.nn.silu(gate_part)
    inner = (activated * up_part).astype(jnp.bfloat16)
    d_down_w = jnp.einsum("nlsf,nlsd->lfd", inner, shaped_grads, preferred_element_type=jnp.float32)
    d_inner = jnp.einsum("nlsd,lfd->nlsf", shaped_grads, w_down, preferred_element_type=jnp.float32)
    d_gate_part = (d_inner * up_part * sigmoid * (1.0 + gate_part * (1.0 - sigmoid))).astype(
        jnp.bfloat16
    )
    d_up_part = (d_inner * activated).astype(jnp.bfloat16)
    d_gate_w = jnp.einsum(
        "nlsd,nlsf->ldf", shaped_rows, d_gate_part, preferred_element_type=jnp.float32
    )
    d_up_w = jnp.einsum(
        "nlsd,nlsf->ldf", shaped_rows, d_up_part, preferred_element_type=jnp.float32
    )
    d_rows = jnp.einsum("nlsf,ldf->nlsd", d_gate_part, w_gate, preferred_element_type=jnp.float32)
    d_rows = d_rows + jnp.einsum(
        "nlsf,ldf->nlsd", d_up_part, w_up, preferred_element_type=jnp.float32
    )
    return (d_rows.astype(jnp.bfloat16).reshape(expert_rows.shape), d_gate_w, d_up_w, d_down_w)


def body(
    tokens,
    prefix,
    routes,
    cotangent,
    w_query,
    key_weight,
    value_weight,
    w_out,
    norm_attn,
    norm_moe,
    w_router,
    w_gate,
    w_up,
    w_down,
):
    inputs = tokens.astype(jnp.float32)
    prefix_len = prefix[0]
    count_of_rows = inputs.shape[0]

    def gather_layer():
        return (
            lax.all_gather(w_query, "shard", axis=0, tiled=True),
            lax.all_gather(key_weight, "shard", axis=0, tiled=True),
            lax.all_gather(value_weight, "shard", axis=0, tiled=True),
            lax.all_gather(w_out, "shard", axis=0, tiled=True),
            lax.all_gather(norm_attn, "shard", axis=0, tiled=True),
            lax.all_gather(norm_moe, "shard", axis=0, tiled=True),
            lax.all_gather(w_router, "shard", axis=0, tiled=True),
        )

    layer_weights = gather_layer()
    state = token_front(layer_weights, inputs, prefix_len, routes)
    expert_rows = lax.all_to_all(state[15], "shard", split_axis=0, concat_axis=0, tiled=True)
    gate_part, up_part, output = expert_forward(expert_rows, w_gate, w_up, w_down)
    returned_rows = lax.all_to_all(output, "shard", split_axis=0, concat_axis=0, tiled=True)
    routed = returned_rows.reshape(EXPERTS * CAP, MODEL_WIDTH)[state[14]].reshape(
        count_of_rows, TOP, MODEL_WIDTH
    )
    mixture = jnp.sum(state[13][:, :, None] * routed.astype(jnp.float32), axis=1)
    result = (state[9] + branch_scale * mixture).astype(jnp.bfloat16)
    grad_out = cotangent.astype(jnp.float32)
    layer_weights = gather_layer()
    state = token_front(layer_weights, inputs, prefix_len, routes)
    (
        scale_one,
        first_normed,
        cosine_table,
        sine_table,
        query_matrix,
        key_rows,
        value_rows,
        log_sums,
        attended,
        hidden_one,
        scale_two,
        normed_two,
        route_picks,
        route_gates,
        places,
        dispatched,
    ) = state
    w_query_all, w_key_all, w_value_all, w_out_all, norm_attn_all, norm_moe_all, w_router_all = (
        layer_weights
    )
    d_mixture = branch_scale * grad_out
    route_grads = (
        (route_gates[:, :, None] * d_mixture[:, None, :])
        .astype(jnp.bfloat16)
        .reshape(count_of_rows * TOP, MODEL_WIDTH)
    )
    grad_rows = (
        jnp.zeros((EXPERTS * CAP, MODEL_WIDTH), jnp.bfloat16)
        .at[places]
        .set(route_grads)
        .reshape(EXPERTS, CAP, MODEL_WIDTH)
    )
    expert_rows, expert_grads = (
        lax.all_to_all(dispatched, "shard", split_axis=0, concat_axis=0, tiled=True),
        lax.all_to_all(grad_rows, "shard", split_axis=0, concat_axis=0, tiled=True),
    )
    gate_part, up_part, output = expert_forward(expert_rows, w_gate, w_up, w_down)
    d_rows, d_gate_w, d_up_w, d_down_w = expert_backward(
        expert_rows, expert_grads, gate_part, up_part, w_gate, w_up, w_down
    )
    back_rows, returned_again = (
        lax.all_to_all(d_rows, "shard", split_axis=0, concat_axis=0, tiled=True),
        lax.all_to_all(output, "shard", split_axis=0, concat_axis=0, tiled=True),
    )
    routed = returned_again.reshape(EXPERTS * CAP, MODEL_WIDTH)[places].reshape(
        count_of_rows, TOP, MODEL_WIDTH
    )
    d_gates = jnp.sum(d_mixture[:, None, :] * routed.astype(jnp.float32), axis=2)
    d_chosen = route_gates * (d_gates - jnp.sum(route_gates * d_gates, axis=1, keepdims=True))
    d_logits = jnp.sum(route_picks * d_chosen[:, :, None], axis=1).astype(jnp.bfloat16)
    d_router_w = outer_sum(normed_two, d_logits)
    route_inputs = back_rows.reshape(EXPERTS * CAP, MODEL_WIDTH)[places].reshape(
        count_of_rows, TOP, MODEL_WIDTH
    )
    d_normed_two = jnp.sum(route_inputs.astype(jnp.float32), axis=1) + back_product(
        d_logits, w_router_all
    )
    d_hidden_one, d_gain_moe = norm_backward(
        hidden_one, scale_two, norm_moe_all.astype(jnp.float32), d_normed_two
    )
    d_hidden_one = d_hidden_one + grad_out
    d_projected = (branch_scale * d_hidden_one).astype(jnp.bfloat16)
    d_out_w = outer_sum(attended, d_projected)
    d_attended = (
        back_product(d_projected, w_out_all).astype(jnp.bfloat16).reshape(query_matrix.shape)
    )
    d_query, key_gradient, value_gradient = attention_backward(
        query_matrix, key_rows, value_rows, d_attended, log_sums, prefix_len
    )
    d_query = (
        apply_rotary(
            d_query.reshape(count_of_rows, QUERY_HEADS, HEAD_SIZE), cosine_table, -sine_table
        )
        .reshape(count_of_rows, QUERY_HEADS * HEAD_SIZE)
        .astype(jnp.bfloat16)
    )
    key_gradient = (
        apply_rotary(key_gradient, cosine_table, -sine_table)
        .reshape(count_of_rows, KEY_VALUE_HEADS * HEAD_SIZE)
        .astype(jnp.bfloat16)
    )
    value_gradient = value_gradient.reshape(count_of_rows, KEY_VALUE_HEADS * HEAD_SIZE).astype(
        jnp.bfloat16
    )
    d_query_w = outer_sum(first_normed, d_query)
    d_key_w = outer_sum(first_normed, key_gradient)
    d_value_w = outer_sum(first_normed, value_gradient)
    d_normed_one = (
        back_product(d_query, w_query_all)
        + back_product(key_gradient, w_key_all)
        + back_product(value_gradient, w_value_all)
    )
    d_inputs, d_gain_attn = norm_backward(
        inputs, scale_one, norm_attn_all.astype(jnp.float32), d_normed_one
    )
    d_inputs = d_inputs + d_hidden_one
    shares = (
        lax.psum_scatter(
            d_query_w.astype(jnp.bfloat16), "shard", scatter_dimension=0, tiled=True
        ).astype(jnp.float32),
        lax.psum_scatter(
            d_key_w.astype(jnp.bfloat16), "shard", scatter_dimension=0, tiled=True
        ).astype(jnp.float32),
        lax.psum_scatter(
            d_value_w.astype(jnp.bfloat16), "shard", scatter_dimension=0, tiled=True
        ).astype(jnp.float32),
        lax.psum_scatter(
            d_out_w.astype(jnp.bfloat16), "shard", scatter_dimension=0, tiled=True
        ).astype(jnp.float32),
        lax.psum_scatter(
            d_gain_attn.astype(jnp.bfloat16), "shard", scatter_dimension=0, tiled=True
        ).astype(jnp.float32),
        lax.psum_scatter(
            d_gain_moe.astype(jnp.bfloat16), "shard", scatter_dimension=0, tiled=True
        ).astype(jnp.float32),
        lax.psum_scatter(
            d_router_w.astype(jnp.bfloat16), "shard", scatter_dimension=0, tiled=True
        ).astype(jnp.float32),
    )
    totals = (
        lax.psum(shares[0].astype(jnp.bfloat16), "rep").astype(jnp.float32),
        lax.psum(shares[1].astype(jnp.bfloat16), "rep").astype(jnp.float32),
        lax.psum(shares[2].astype(jnp.bfloat16), "rep").astype(jnp.float32),
        lax.psum(shares[3].astype(jnp.bfloat16), "rep").astype(jnp.float32),
        lax.psum(shares[4].astype(jnp.bfloat16), "rep").astype(jnp.float32),
        lax.psum(shares[5].astype(jnp.bfloat16), "rep").astype(jnp.float32),
        lax.psum(shares[6].astype(jnp.bfloat16), "rep").astype(jnp.float32),
        lax.psum(d_gate_w.astype(jnp.bfloat16), "rep").astype(jnp.float32),
        lax.psum(d_up_w.astype(jnp.bfloat16), "rep").astype(jnp.float32),
        lax.psum(d_down_w.astype(jnp.bfloat16), "rep").astype(jnp.float32),
    )
    return (
        result,
        d_inputs,
        totals[0],
        totals[1],
        totals[2],
        totals[3],
        totals[4],
        totals[5],
        totals[6],
        totals[7],
        totals[8],
        totals[9],
    )


def solution(mesh):
    placed = (
        P(("rep", "shard"), None),
        P(("rep", "shard")),
        P(("rep", "shard"), None),
        P(("rep", "shard"), None),
        P("shard", None),
        P("shard", None),
        P("shard", None),
        P("shard", None),
        P("shard"),
        P("shard"),
        P("shard", None),
        P("shard", None, None),
        P("shard", None, None),
        P("shard", None, None),
    )
    return jax.shard_map(
        body,
        mesh=mesh,
        in_specs=placed,
        out_specs=(
            P(("rep", "shard"), None),
            P(("rep", "shard"), None),
            P("shard", None),
            P("shard", None),
            P("shard", None),
            P("shard", None),
            P("shard"),
            P("shard"),
            P("shard", None),
            P("shard", None, None),
            P("shard", None, None),
            P("shard", None, None),
        ),
        check_vma=False,
    )
```

profile of v0, /device:TPU:0, one launch (start us, length us, event | category | flops | bytes accessed | tf_op | source)
XLA Modules:
  0.0 1203.6 jit_solution(14482594480034760632)
XLA Ops:
  14.2 9.1 reduce-window.6
  24.2 10.2 all-gather
  34.4 8.7 all-gather.1
  45.6 16.0 %all-gather.9.cloned.1.call-done = bf16[1024,512]{1,0:T(8,128)(2,1)} async-done(((bf16[128,512]{1,0:T(8,128)(2,1)}), bf16[1024,512]{1,0:T(8,128)(2,1)}) %all-gather.9.cloned.1.call-update) | async-done | bytes 1048592 | tf_op jit(solution)/shard_map/all_gather | solution.py:287
  63.6 27.9 %all-gather.11.cloned.1.call-done = bf16[1024,1024]{1,0:T(8,128)(2,1)} async-done(((bf16[128,1024]{1,0:T(8,128)(2,1)}), bf16[1024,1024]{1,0:T(8,128)(2,1)}) %all-gather.11.cloned.1.call-update) | async-done | bytes 2097168 | tf_op jit(solution)/shard_map/all_gather | solution.py:286
  91.5 2.6 fusion.100
  98.8 22.4 %all-gather.13.cloned.1.call-done = bf16[1024,1024]{1,0:T(8,128)(2,1)} async-done(((bf16[128,1024]{1,0:T(8,128)(2,1)}), bf16[1024,1024]{1,0:T(8,128)(2,1)}) %all-gather.13.cloned.1.call-update) | async-done | bytes 2097168 | tf_op jit(solution)/shard_map/all_gather | solution.py:289
  121.1 2.4 multiply_reduce_fusion.2
  123.8 13.8 %scatter_custom_fusion = bf16[3072,1024]{1,0:T(8,128)(2,1)} fusion(s32[2048]{0:T(1024)S(1)} %bitcast.273, bf16[]{:T(256)} %constant.93.clone.1, bf16[256,1024]{1,0:T(8,128)(2,1)S(1)} %multiply_convert_fusion.1), kind=kCustom, calls=%fused_computation.56 | custom fusion | bytes 6815746 | tf_op jit(solution)/shard_map/scatter | solution.py:191
  137.6 4.8 all-to-all-start
  142.4 74.6 %all_gather.34 = bf16[1024,32]{0,1:T(8,128)(2,1)S(1)} all-gather(bf16[128,32]{0,1:T(8,128)(2,1)S(1)} %copy-done.20), channel_id=1, replica_groups=mesh['rep'=4,'shard'=8] {'shard'}, dimensions={0}, use_global_device_ids=true | all-gather | bytes 73728 | tf_op jit(solution)/shard_map/all_gather | solution.py:292
  218.8 14.4 %scatter_custom_fusion.1 = bf16[3072,1024]{1,0:T(8,128)(2,1)} fusion(s32[2048]{0:T(1024)S(1)} %bitcast.274, f32[256,1024]{1,0:T(8,128)S(1)} %convert_multiply_fusion.7, f32[2048]{0:T(1024)S(1)} %div.71, bf16[]{:T(256)} %constant.93.clone.1), kind=kCustom, calls=%fused_computation.41 | custom fusion | flops 4194304 | bytes 7348226 | tf_op jit(solution)/shard_map/scatter | solution.py:338
  233.2 5.0 all-to-all-start.2
  238.3 10.3 fusion.18
  248.5 8.1 fusion.20
  256.6 53.2 %all-to-all-done.2 = bf16[32,96,1024]{2,1,0:T(8,128)(2,1)} async-done(((bf16[32,96,1024]{2,1,0:T(8,128)(2,1)}), bf16[32,96,1024]{2,1,0:T(8,128)(2,1)}, u32[]{:S(2)}, u32[]{:S(2)}) %all-to-all-start.2) | async-done | bytes 6291488 | tf_op jit(solution)/shard_map/all_to_all | solution.py:343
  309.9 13.1 %fusion.7 = (bf16[8,4,96,512]{3,2,0,1:T(8,128)(2,1)}, bf16[8,4,96,512]{3,2,0,1:T(8,128)(2,1)}, bf16[8,4,96,512]{3,2,0,1:T(8,128)(2,1)}) fusion(f32[4,8,96,512]{3,2,1,0:T(8,128)} %fusion.18, f32[4,8,96,512]{3,2,1,0:T(8,128)} %fusion.20, bf16[4,512,1024]{2,1,0:T(8,128)(2,1)} %param.27, bf16[8,4,96,1024]{3,2,1,0:T(8,128)(2,1)} %bitcast.41), kind=kOutput, calls=%fused_computation.21 | convolution fusion | flops 3244818432 | bytes 32505856 | tf_op jit(solution)/shard_map/nlsd,lfd->nlsf/dot_general | solution.py:246
  323.0 5.6 convert_bitcast_fusion
  328.6 3.4 copy.125
  332.0 5.3 all-to-all-start.1
  337.3 11.2 fusion.27
  348.4 12.9 %fusion.4 = bf16[8,4,96,1024]{3,2,0,1:T(8,128)(2,1)} fusion(f32[4,8,96,1024]{3,2,1,0:T(8,128)} %fusion.27, bf16[8,4,96,512]{3,2,0,1:T(8,128)(2,1)} %get-tuple-element.99, bf16[4,1024,512]{2,1,0:T(8,128)(2,1)} %param.25), kind=kOutput, calls=%fused_computation.16 | convolution fusion | flops 3227516928 | bytes 26214400 | tf_op jit(solution)/shard_map/nlsf,ldf->nlsd/dot_general | solution.py:257
  361.4 6.6 copy.128
  368.0 40.9 %all-to-all-done.1 = bf16[32,96,1024]{2,1,0:T(8,128)(2,1)} async-done(((bf16[32,96,1024]{2,1,0:T(8,128)(2,1)}), bf16[32,96,1024]{2,1,0:T(8,128)(2,1)}, u32[]{:S(2)}, u32[]{:S(2)}) %all-to-all-start.1) | async-done | bytes 6291488 | tf_op jit(solution)/shard_map/all_to_all | solution.py:299
  408.9 4.7 all-to-all-start.3
  413.9 14.5 %gather_fusion = bf16[2048,1024]{1,0:T(8,128)(2,1)} fusion(bf16[3072,1024]{1,0:T(8,128)(2,1)} %bitcast.34, s32[2048]{0:T(1024)S(1)} %broadcast_clamp_fusion), kind=kCustom, calls=%fused_computation | custom fusion | bytes 8396800 | tf_op jit(solution)/shard_map/gather | solution.py:300
  428.4 6.1 fusion.2
  435.6 49.6 %all-to-all-done.3 = bf16[32,96,1024]{2,1,0:T(8,128)(2,1)} async-done(((bf16[32,96,1024]{2,1,0:T(8,128)(2,1)}), bf16[32,96,1024]{2,1,0:T(8,128)(2,1)}, u32[]{:S(2)}, u32[]{:S(2)}) %all-to-all-start.3) | async-done | bytes 6291488 | tf_op jit(solution)/shard_map/all_to_all | solution.py:350
  485.2 14.5 %gather_fusion.1 = bf16[2048,1024]{1,0:T(8,128)(2,1)} fusion(bf16[3072,1024]{1,0:T(8,128)(2,1)} %bitcast.48, s32[2048]{0:T(1024)S(1)} %broadcast_clamp_fusion), kind=kCustom, calls=%fused_computation.1 | custom fusion | bytes 8396800 | tf_op jit(solution)/shard_map/gather | solution.py:360
  499.7 5.6 convert_reduce_fusion
  508.1 3.0 fusion.65
  513.0 3.7 fusion.107
  516.7 8.9 fusion.61
  530.6 8.8 fusion.57
  543.1 9.3 bitcast_convert_fusion.2
  552.4 7.8 bitcast_convert_fusion
  561.6 9.3 bitcast_convert_fusion.1
  570.9 16.2 %reduce-scatter.10.cloned.1.call-done = bf16[128,512]{1,0:T(8,128)(2,1)} async-done(((bf16[1024,512]{1,0:T(8,128)(2,1)}), bf16[128,512]{1,0:T(8,128)(2,1)}) %reduce-scatter.10.cloned.1.call-update) | async-done | bytes 131088 | tf_op jit(solution)/shard_map/reduce_scatter | solution.py:409
  587.1 44.5 %reduce-scatter.14.cloned.1.call-done = bf16[128,1024]{1,0:T(8,128)(2,1)} async-done(((bf16[1024,1024]{1,0:T(8,128)(2,1)}), bf16[128,1024]{1,0:T(8,128)(2,1)}) %reduce-scatter.14.cloned.1.call-update) | async-done | bytes 262160 | tf_op jit(solution)/shard_map/reduce_scatter | solution.py:415
  631.6 44.9 %reduce-scatter.8.cloned.1.call-done = bf16[128,1024]{1,0:T(8,128)(2,1)} async-done(((bf16[1024,1024]{1,0:T(8,128)(2,1)}), bf16[128,1024]{1,0:T(8,128)(2,1)}) %reduce-scatter.8.cloned.1.call-update) | async-done | bytes 262160 | tf_op jit(solution)/shard_map/reduce_scatter | solution.py:406
  678.4 2.5 fusion.108
  682.2 12.7 %all-reduce.2 = (bf16[1024]{0:T(1024)(128)(2,1)S(1)}, bf16[1024]{0:T(1024)(128)(2,1)S(1)}) all-reduce(bf16[1024]{0:T(1024)(128)(2,1)S(1)} %get-tuple-element.75, bf16[1024]{0:T(1024)(128)(2,1)S(1)} %get-tuple-element.73), channel_id=6, replica_groups=mesh['rep'=4,'shard'=8] {'shard'}, use_global_device_ids=true, to_apply=%region_29.30.clone | all-reduce | flops 2048 | bytes 8192
  696.3 17.5 %reduce-scatter.16.cloned.1.call-done = bf16[128,32]{1,0:T(8,128)(2,1)} async-done(((bf16[1024,32]{1,0:T(8,128)(2,1)}), bf16[128,32]{1,0:T(8,128)(2,1)}) %reduce-scatter.16.cloned.1.call-update) | async-done | bytes 8208
  714.6 12.1 %all-reduce.3 = (bf16[128]{0:T(256)(128)(2,1)S(1)}, bf16[128]{0:T(256)(128)(2,1)S(1)}, bf16[128,32]{0,1:T(8,128)(2,1)S(1)}) all-reduce(bf16[128]{0:T(256)(128)(2,1)S(1)} %dynamic-slice.3, bf16[128]{0:T(256)(128)(2,1)S(1)} %dynamic-slice.5, bf16[128,32]{0,1:T(8,128)(2,1)S(1)} %copy.154), channel_id=1, replica_groups=mesh['rep'=4,'shard'=8] {'rep'}, use_global_device_ids=true, to_apply=%region_30.31 | all-reduce | flops 4352 | bytes 17408 | tf_op jit(solution)/shard_map/psum | solution.py:433
  728.3 445.2 %all-reduce.7.cloned.1.call-done = (bf16[128,1024]{1,0:T(8,128)(2,1)}, bf16[128,512]{1,0:T(8,128)(2,1)}, bf16[128,512]{1,0:T(8,128)(2,1)}, bf16[128,1024]{1,0:T(...) async-done(((bf16[128,1024]{1,0:T(8,128)(2,1)}, bf16[128,512]{1,0:T(8,128)(2,1)}, ...) | async-done | bytes 13369360 | tf_op jit(solution)/shard_map/psum | solution.py:429
  1180.3 6.9 convert_element_type.273
  1187.3 4.6 convert_element_type.275
  1191.8 4.4 convert_element_type.277
  (153 shorter events, 47.1 us)
Async XLA Ops:
  7.2 36.6 %copy-start.1 = (bf16[256,1024]{1,0:T(8,128)(2,1)S(1)}, bf16[256,1024]{1,0:T(8,128)(2,1)}, u32[]{:S(2)}) copy-start(bf16[256,1024]{1,0:T(8,128)(2,1)} %param.14) | copy-start | bytes 1572868
  7.2 17.0 %copy-start.22 = (bf16[128]{0:T(256)(128)(2,1)S(1)}, bf16[128]{0:T(256)(128)(2,1)}, u32[]{:S(2)}) copy-start(bf16[128]{0:T(256)(128)(2,1)} %param.22) | copy-start | bytes 772
  7.2 27.2 %copy-start.23 = (bf16[128]{0:T(256)(128)(2,1)S(1)}, bf16[128]{0:T(256)(128)(2,1)}, u32[]{:S(2)}) copy-start(bf16[128]{0:T(256)(128)(2,1)} %param.23) | copy-start | bytes 772
  7.2 36.5 %all-gather.7.cloned.1.call-start = ((), (), s32[]{:S(2)}) async-start(), calls=%async_computation.9 | async-start | bytes 1179648 | tf_op jit(solution)/shard_map/all_gather | solution.py:288
  7.9 53.7 %all-gather.9.cloned.1.call-start = ((), (), s32[]{:S(2)}) async-start(), calls=%async_computation.10 | async-start | bytes 1179648 | tf_op jit(solution)/shard_map/all_gather | solution.py:287
  8.7 82.8 %all-gather.11.cloned.1.call-start = ((), (), s32[]{:S(2)}) async-start(), calls=%async_computation.11 | async-start | bytes 2359296 | tf_op jit(solution)/shard_map/all_gather | solution.py:286
  9.4 111.7 %all-gather.13.cloned.1.call-start = ((), (), s32[]{:S(2)}) async-start(), calls=%async_computation.12 | async-start | bytes 2359296 | tf_op jit(solution)/shard_map/all_gather | solution.py:289
  45.6 50.9 %copy-start.12 = (bf16[256,512]{0,1:T(8,128)(2,1)}, bf16[256,512]{0,1:T(8,128)(2,1)S(1)}, u32[]{:S(2)}) copy-start(bf16[256,512]{0,1:T(8,128)(2,1)S(1)} %copy.113) | copy-start | bytes 786436
  63.6 32.3 %copy-start.15 = (bf16[256,8,32]{0,2,1:T(8,128)(2,1)}, bf16[256,8,32]{0,2,1:T(8,128)(2,1)S(1)}, u32[]{:S(2)}) copy-start(bf16[256,8,32]{0,2,1:T(8,128)(2,1)S(1)} %get-tuple-element.110) | copy-start | bytes 393220
  63.6 32.3 %copy-start.17 = (bf16[256,8,32]{0,2,1:T(8,128)(2,1)}, bf16[256,8,32]{0,2,1:T(8,128)(2,1)S(1)}, u32[]{:S(2)}) copy-start(bf16[256,8,32]{0,2,1:T(8,128)(2,1)S(1)} %get-tuple-element.111) | copy-start | bytes 393220
  94.3 0.8 copy-start.10
  95.9 2.0 copy-start
  98.7 38.8 %copy-start.8 = (bf16[8,64,2,256]{3,1,2,0:T(8,128)(2,1)}, bf16[8,64,2,256]{3,1,2,0:T(8,128)(2,1)S(1)}, u32[]{:S(2)}) copy-start(bf16[8,64,2,256]{3,1,2,0:T(8,128)(2,1)S(1)} %fusion.60) | copy-start | bytes 1572868
  137.6 4.8 copy-start.20
  137.6 80.9 %copy-start.19 = (s32[256,8]{0,1:T(8,128)S(1)}, s32[256,8]{0,1:T(8,128)}, u32[]{:S(2)}) copy-start(s32[256,8]{0,1:T(8,128)} %param.16) | copy-start | bytes 24580
  137.6 95.6 %all-to-all-start = ((bf16[32,96,1024]{2,1,0:T(8,128)(2,1)}), bf16[32,96,1024]{2,1,0:T(8,128)(2,1)}, u32[]{:S(2)}, u32[]{:S(2)}) async-start(bf16[32,96,1024]{2,1,0:T(8,128)(2,1)} %bitcast.233), calls=%async_computation | async-start | bytes 12582912 | tf_op jit(solution)/shard_map/all_to_all | solution.py:297
  233.2 76.6 %all-to-all-start.2 = ((bf16[32,96,1024]{2,1,0:T(8,128)(2,1)}), bf16[32,96,1024]{2,1,0:T(8,128)(2,1)}, u32[]{:S(2)}, u32[]{:S(2)}) async-start(bf16[32,96,1024]{2,1,0:T(8,128)(2,1)} %bitcast.234), calls=%async_computation.2 | async-start | bytes 12582912 | tf_op jit(solution)/shard_map/all_to_all | solution.py:343
  238.3 10.3 copy-start.3
  309.9 13.2 %copy-start.24 = (bf16[4,512,1024]{2,1,0:T(8,128)(2,1)S(1)}, bf16[4,512,1024]{2,1,0:T(8,128)(2,1)}, u32[]{:S(2)}) copy-start(bf16[4,512,1024]{2,1,0:T(8,128)(2,1)} %param.27) | copy-start | bytes 12582916
  332.0 76.9 %all-to-all-start.1 = ((bf16[32,96,1024]{2,1,0:T(8,128)(2,1)}), bf16[32,96,1024]{2,1,0:T(8,128)(2,1)}, u32[]{:S(2)}, u32[]{:S(2)}) async-start(bf16[32,96,1024]{2,1,0:T(8,128)(2,1)} %bitcast.235), calls=%async_computation.1 | async-start | bytes 12582912 | tf_op jit(solution)/shard_map/all_to_all | solution.py:299
  408.9 76.3 %all-to-all-start.3 = ((bf16[32,96,1024]{2,1,0:T(8,128)(2,1)}), bf16[32,96,1024]{2,1,0:T(8,128)(2,1)}, u32[]{:S(2)}, u32[]{:S(2)}) async-start(bf16[32,96,1024]{2,1,0:T(8,128)(2,1)} %bitcast.232), calls=%async_computation.3 | async-start | bytes 12582912 | tf_op jit(solution)/shard_map/all_to_all | solution.py:350
  413.6 157.2 %reduce-scatter.12.cloned.1.call-start = ((), (), s32[]{:S(2)}) async-start(), calls=%async_computation.15 | async-start | bytes 1179648 | tf_op jit(solution)/shard_map/reduce_scatter | solution.py:412
  499.7 6.2 copy-start.6
  499.7 6.2 copy-start.7
  505.3 1.8 copy-start.2
  511.1 5.7 copy-start.11
  512.8 74.3 %reduce-scatter.10.cloned.1.call-start = ((), (), s32[]{:S(2)}) async-start(), calls=%async_computation.14 | async-start | bytes 1179648 | tf_op jit(solution)/shard_map/reduce_scatter | solution.py:409
  516.7 11.7 copy-start.9
  526.8 3.9 copy-start.16
  526.8 3.9 copy-start.18
  528.4 103.2 %reduce-scatter.14.cloned.1.call-start = ((), (), s32[]{:S(2)}) async-start(), calls=%async_computation.16 | async-start | bytes 2359296 | tf_op jit(solution)/shard_map/reduce_scatter | solution.py:415
  530.6 146.0 %reduce-scatter.8.cloned.1.call-start = ((), (), s32[]{:S(2)}) async-start(), calls=%async_computation.13 | async-start | bytes 2359296 | tf_op jit(solution)/shard_map/reduce_scatter | solution.py:406
  543.0 170.8 %reduce-scatter.16.cloned.1.call-start = ((), (), s32[]{:S(2)}) async-start(), calls=%async_computation.17 | async-start | bytes 294912
  543.1 9.3 copy-start.26
  561.3 612.2 %all-reduce.7.cloned.1.call-start = ((), (), s32[]{:S(2)}) async-start(), calls=%async_computation.18 | async-start | bytes 26738688 | tf_op jit(solution)/shard_map/psum | solution.py:429
  676.5 0.7 copy-start.25
  678.4 2.5 copy-start.13
  678.4 3.0 copy-start.14
  681.0 14.1 %copy-start.21 = (f32[256]{0:T(256)S(1)}, f32[256]{0:T(256)}, u32[]{:S(2)}) copy-start(f32[256]{0:T(256)} %get-tuple-element.112) | copy-start | bytes 3076
  1180.3 6.9 copy-start.5
  1187.2 4.6 copy-start.4
Sparse Core Ops, SparseCore 0:
  9.9 26.2 all-gather.6
  38.1 23.5 all-gather.8
  63.5 27.8 all-gather.10
  93.2 27.8 all-gather.12
  512.9 35.1 reduce-scatter.11
  551.1 35.9 reduce-scatter.9
  590.4 41.1 reduce-scatter.13
  635.3 41.2 reduce-scatter.7
  680.1 33.5 reduce-scatter.15
  718.0 455.3 all-reduce.6
where the time goes:
time: 1210 us; the launch traced here: 1200 us
  waiting for transfers between devices  781 us (65%)
  matrix products  135 us (11%)
  blocking collectives  118 us (10%)
  other arithmetic  70.3 us (6%)
  local copies, waits for them, and re-layouts  61.4 us (5%)
  starting transfers between devices  20.9 us (2%)
  between operations  16.5 us (1%)
    psum x1, waiting for transfers between devices, body(): lax.psum(shares[0].astype(jnp.bfloat16), 'rep').astype(jnp.float32)  445 us
    all_gather x1, blocking collectives, gather_layer(): lax.all_gather(w_router, 'shard', axis=0, tiled=True)  74.6 us
    all_to_all x1, waiting for transfers between devices, body(): lax.all_to_all(grad_rows, 'shard', split_axis=0, concat_axis=0, tiled=True)  53.2 us
    all_to_all x1, waiting for transfers between devices, body(): lax.all_to_all(d_rows, 'shard', split_axis=0, concat_axis=0, tiled=True)  49.6 us
    reduce_scatter x1, waiting for transfers between devices, body(): lax.psum_scatter(d_query_w.astype(jnp.bfloat16), 'shard', scatter_dimensi...  44.9 us
    reduce_scatter x1, waiting for transfers between devices, body(): lax.psum_scatter(d_out_w.astype(jnp.bfloat16), 'shard', scatter_dimension...  44.5 us
    all_to_all x1, waiting for transfers between devices, body(): lax.all_to_all(output, 'shard', split_axis=0, concat_axis=0, tiled=True)  40.9 us
    all_gather x1, waiting for transfers between devices, gather_layer(): lax.all_gather(w_query, 'shard', axis=0, tiled=True)  27.9 us
  transfers between devices with their start and end apart: 14, of which 11 were waited for; matrix products, arithmetic and copies ran while one was open for 15% of the time, Pallas kernels for 0%

commit v1 on v0

v1 whole, which is shorter than its diff:
```python
import math

import jax
import jax.numpy as jnp
from jax import lax
from jax.sharding import PartitionSpec as P

QUERY_HEADS = 16
KEY_VALUE_HEADS = 8
HEAD_SIZE = 64
CAP = 96
LANES = 128
MOST_GATHERED = 4

epsilon = 1e-06
score_scale = 0.015625
branch_scale = 0.22
masked_value = -1e30

f32 = jnp.float32
bf16 = jnp.bfloat16


def dot(left, right, contract=((1,), (0,))):
    return lax.dot_general(left, right, (contract, ((), ())), preferred_element_type=f32)


def norm_scale(rows):
    return lax.rsqrt(jnp.mean(rows * rows, axis=-1, keepdims=True) + epsilon)


def norm_backward(rows, scaling, gain, upstream):
    weighted = upstream * gain
    inner_mean = jnp.mean(weighted * rows, axis=-1, keepdims=True)
    gradient = scaling * weighted - rows * (scaling * scaling * scaling) * inner_mean
    return gradient, jnp.sum(upstream * rows * scaling, axis=0, keepdims=True)


def rotary_tables(count):
    half = HEAD_SIZE // 2
    places = jnp.arange(count, dtype=f32)
    inverse = jnp.exp(jnp.arange(half, dtype=f32) * (-2.0 * math.log(10000.0) / HEAD_SIZE))
    angles = places[:, None] * inverse[None, :]
    return jnp.cos(angles)[:, None, :], jnp.sin(angles)[:, None, :]


def apply_rotary(rows, cosine, sine):
    half = HEAD_SIZE // 2
    shaped = rows.reshape(rows.shape[0], -1, HEAD_SIZE)
    first, second = shaped[..., :half], shaped[..., half:]
    turned = jnp.concatenate(
        [first * cosine - second * sine, second * cosine + first * sine], axis=-1
    )
    return turned.reshape(rows.shape)


def attention_scores(query, keys, prefix_len):
    count = query.shape[0]
    raw = jnp.einsum("tngd,snd->ngts", query, keys, preferred_element_type=f32)
    place = jnp.arange(count, dtype=jnp.int32)
    visible = (place[None, :] <= place[:, None]) | (place[None, :] < prefix_len)
    return jnp.where(visible, raw * score_scale, masked_value)


def slots_of(gates, first_expert, local):
    tokens = gates.shape[1]
    mine = lax.dynamic_slice_in_dim(gates, first_expert, local, axis=2)
    named = mine > 0
    place = jnp.arange(tokens)
    earlier = (place[None, :] < place[:, None]).astype(bf16)
    rank = jnp.einsum("ts,bsl->blt", earlier, named.astype(bf16), preferred_element_type=f32)
    slot = jnp.arange(CAP, dtype=f32)
    here = (rank[:, :, None, :] == slot[None, None, :, None]) & named.transpose(0, 2, 1)[:, :, None, :]
    return here, mine


def body(
    tokens, prefix, routes, cotangent, w_query, key_weight, value_weight, w_out,
    norm_attn, norm_moe, w_router, w_gate, w_up, w_down,
):
    inputs = tokens.astype(f32)
    count, width = inputs.shape
    local, _, hidden = w_gate.shape
    shards, reps = lax.axis_size("shard"), lax.axis_size("rep")
    experts = local * shards
    kv_width = key_weight.shape[1]
    me, rep = lax.axis_index("shard"), lax.axis_index("rep")
    group = QUERY_HEADS // KEY_VALUE_HEADS

    small = jnp.concatenate([w_router, norm_attn[:, None], norm_moe[:, None]], axis=1)
    small = jnp.pad(small, ((0, 0), (0, LANES - small.shape[1])))
    packed = jnp.concatenate([w_query, key_weight, value_weight, w_out, small], axis=1)
    packed = lax.all_gather(packed, "shard", axis=0, tiled=True)
    cuts = [width, width + kv_width, width + 2 * kv_width, 2 * width + 2 * kv_width]
    wq, wk, wv, wo, small = jnp.split(packed, cuts, axis=1)
    wr = small[:, :experts]
    gain_one = small[:, experts].astype(f32)[None, :]
    gain_two = small[:, experts + 1].astype(f32)[None, :]
    spread = reps <= MOST_GATHERED
    axes = ("rep", "shard") if spread else "shard"
    all_cot = lax.all_gather(cotangent, axes, axis=0, tiled=True)

    scale_one = norm_scale(inputs)
    normed_one = (inputs * scale_one * gain_one).astype(bf16)
    cosine, sine = rotary_tables(count)
    query = apply_rotary(dot(normed_one, wq), cosine, sine).astype(bf16)
    keys = apply_rotary(dot(normed_one, wk), cosine, sine).astype(bf16)
    values = dot(normed_one, wv).astype(bf16)
    query4 = query.reshape(count, KEY_VALUE_HEADS, group, HEAD_SIZE)
    keys3 = keys.reshape(count, KEY_VALUE_HEADS, HEAD_SIZE)
    values3 = values.reshape(count, KEY_VALUE_HEADS, HEAD_SIZE)
    scores = attention_scores(query4, keys3, prefix[0])
    weights = jnp.exp(scores - jnp.max(scores, axis=-1, keepdims=True))
    probs = weights / jnp.sum(weights, axis=-1, keepdims=True)
    probs_low = probs.astype(bf16)
    attended = jnp.einsum("ngts,snd->tngd", probs_low, values3, preferred_element_type=f32)
    attended = attended.reshape(count, -1).astype(bf16)
    hidden_one = inputs + branch_scale * dot(attended, wo)
    scale_two = norm_scale(hidden_one)
    normed_two = (hidden_one * scale_two * gain_two).astype(bf16)
    logits = dot(normed_two, wr)
    picks = routes[:, :, None] == jnp.arange(experts, dtype=jnp.int32)[None, None, :]
    chosen_mask = jnp.any(picks, axis=1)
    top = jnp.max(jnp.where(chosen_mask, logits, -jnp.inf), axis=1, keepdims=True)
    gates = jnp.where(chosen_mask, jnp.exp(logits - top), 0.0)
    gates = gates / jnp.sum(gates, axis=1, keepdims=True)

    high = gates.astype(bf16)
    low = (gates - high.astype(f32)).astype(bf16)
    pad = jnp.zeros((count, LANES - 2 * experts), bf16)
    sent = jnp.concatenate([normed_two, high, low, pad], axis=1)
    arrived = lax.all_gather(sent, axes, axis=0, tiled=True)
    arrived = arrived.reshape(-1, shards, count, width + LANES)
    all_gates = arrived[..., width : width + experts].astype(f32)
    all_gates = all_gates + arrived[..., width + experts : width + 2 * experts].astype(f32)
    all_cot = all_cot.reshape(-1, shards, count, width)

    def gathered(number):
        rows = lax.dynamic_index_in_dim(arrived, number, 0, keepdims=False)[..., :width]
        cot = lax.dynamic_index_in_dim(all_cot, number, 0, keepdims=False)
        gate_rows = lax.dynamic_index_in_dim(all_gates, number, 0, keepdims=False)
        here, mine = slots_of(gate_rows, me * local, local)
        one_hot = here.astype(bf16)
        slot_gate = jnp.sum(jnp.where(here, mine.transpose(0, 2, 1)[:, :, None, :], 0.0), axis=3)
        xg = jnp.einsum("blst,btd->lbsd", one_hot, rows).reshape(local, -1, width)
        cg = jnp.einsum("blst,btd->lbsd", one_hot, cot).reshape(local, -1, width)
        scale = branch_scale * slot_gate.transpose(1, 0, 2).reshape(local, -1)[:, :, None]
        gate_part = jnp.einsum("lmd,ldf->lmf", xg, w_gate, preferred_element_type=f32)
        up_part = jnp.einsum("lmd,ldf->lmf", xg, w_up, preferred_element_type=f32)
        raw = jnp.einsum("lmd,lfd->lmf", cg, w_down, preferred_element_type=f32)
        sigma = jax.nn.sigmoid(gate_part)
        act = gate_part * sigma
        inner = act * up_part
        d_inner = raw * scale
        d_gate = (d_inner * up_part * sigma * (1.0 + gate_part * (1.0 - sigma))).astype(bf16)
        d_up = (d_inner * act).astype(bf16)
        scaled = (inner * scale).astype(bf16)
        sums = (
            jnp.einsum("lmd,lmf->ldf", xg, d_gate, preferred_element_type=f32),
            jnp.einsum("lmd,lmf->ldf", xg, d_up, preferred_element_type=f32),
            jnp.einsum("lmf,lmd->lfd", scaled, cg, preferred_element_type=f32),
        )
        return sums, (one_hot, inner, raw, d_gate, d_up, scaled)

    sums, (one_hot, inner, raw, d_gate, d_up, scaled) = gathered(rep if spread else 0)
    out_rows = jnp.einsum("lmf,lfd->lmd", scaled, w_down, preferred_element_type=f32).astype(bf16)
    d_rows = jnp.einsum("lmf,ldf->lmd", d_gate, w_gate, preferred_element_type=f32)
    d_rows = (d_rows + jnp.einsum("lmf,ldf->lmd", d_up, w_up, preferred_element_type=f32)).astype(bf16)
    slot_d_gate = branch_scale * jnp.sum(inner * raw, axis=2)
    shape4 = (local, shards, CAP, width)
    mix = jnp.einsum("blst,lbsd->btd", one_hot, out_rows.reshape(shape4), preferred_element_type=f32)
    d_in = jnp.einsum("blst,lbsd->btd", one_hot, d_rows.reshape(shape4), preferred_element_type=f32)
    dg_local = jnp.sum(
        jnp.where(one_hot > 0, slot_d_gate.reshape(local, shards, CAP).transpose(1, 0, 2)[..., None], 0.0), axis=2
    )
    dg = jnp.zeros((shards, count, LANES), f32)
    dg = lax.dynamic_update_slice(dg, dg_local.transpose(0, 2, 1), (0, 0, me * local))
    back = jnp.concatenate([mix, d_in, dg], axis=2).astype(bf16).reshape(shards * count, -1)
    back = lax.psum_scatter(back, "shard", scatter_dimension=0, tiled=True).astype(f32)
    if spread:
        for step in range(1, reps):
            more, _ = gathered(lax.rem(rep + step, reps))
            sums = tuple(a + b for a, b in zip(sums, more))
    else:
        sums = tuple(lax.psum(a.astype(bf16), "rep").astype(f32) for a in sums)
    d_w_gate, d_w_up, d_w_down = sums

    result = (hidden_one + back[:, :width]).astype(bf16)
    cot = cotangent.astype(f32)
    d_gates = back[:, 2 * width : 2 * width + experts]
    d_logits = gates * (d_gates - jnp.sum(gates * d_gates, axis=1, keepdims=True))
    d_logits = d_logits.astype(bf16)
    d_router = dot(normed_two, d_logits, ((0,), (0,)))
    d_normed_two = back[:, width : 2 * width] + dot(d_logits, wr, ((1,), (1,)))
    d_hidden, d_gain_two = norm_backward(hidden_one, scale_two, gain_two, d_normed_two)
    d_hidden = d_hidden + cot
    d_projected = (branch_scale * d_hidden).astype(bf16)
    d_wo = dot(attended, d_projected, ((0,), (0,)))
    d_attended = dot(d_projected, wo, ((1,), (1,))).astype(bf16)
    d_attended = d_attended.reshape(count, KEY_VALUE_HEADS, group, HEAD_SIZE)
    d_values = jnp.einsum("ngts,tngd->snd", probs_low, d_attended, preferred_element_type=f32)
    d_probs = jnp.einsum("tngd,snd->ngts", d_attended, values3, preferred_element_type=f32)
    weighted = jnp.sum(probs * d_probs, axis=-1, keepdims=True)
    d_scores = (probs * (d_probs - weighted) * score_scale).astype(bf16)
    d_query = jnp.einsum("ngts,snd->tngd", d_scores, keys3, preferred_element_type=f32)
    d_keys = jnp.einsum("ngts,tngd->snd", d_scores, query4, preferred_element_type=f32)
    d_query = apply_rotary(d_query.reshape(count, -1), cosine, -sine).astype(bf16)
    d_keys = apply_rotary(d_keys.reshape(count, -1), cosine, -sine).astype(bf16)
    d_values = d_values.reshape(count, -1).astype(bf16)
    d_qkv = jnp.concatenate([d_query, d_keys, d_values], axis=1)
    d_w_qkv = dot(normed_one, d_qkv, ((0,), (0,)))
    d_normed_one = dot(d_qkv, packed[:, : cuts[2]], ((1,), (1,)))
    d_tokens, d_gain_one = norm_backward(inputs, scale_one, gain_one, d_normed_one)
    d_tokens = d_tokens + d_hidden
    small = jnp.concatenate([d_router, d_gain_one.T, d_gain_two.T], axis=1)
    small = jnp.pad(small, ((0, 0), (0, LANES - small.shape[1])))
    shares = jnp.concatenate([d_w_qkv, d_wo, small], axis=1).astype(bf16)
    shares = lax.psum_scatter(shares, "shard", scatter_dimension=0, tiled=True)
    totals = lax.psum(shares, "rep").astype(f32)
    d_wq, d_wk, d_wv, d_wo, small = jnp.split(totals, cuts, axis=1)
    return (
        result, d_tokens, d_wq, d_wk, d_wv, d_wo, small[:, experts], small[:, experts + 1],
        small[:, :experts], d_w_gate, d_w_up, d_w_down,
    )


def solution(mesh):
    rows = P(("rep", "shard"), None)
    one, two, three = P("shard"), P("shard", None), P("shard", None, None)
    return jax.shard_map(
        body,
        mesh=mesh,
        in_specs=(rows, P(("rep", "shard")), rows, rows, two, two, two, two, one, one, two, three, three, three),
        out_specs=(rows, rows, two, two, two, two, one, one, two, three, three, three),
        check_vma=False,
    )
```

time: 1210 us -> 844 us (0.70)
  waiting for transfers between devices: 781 us -> 285 us
  matrix products: 135 us -> 415 us
  blocking collectives: 118 us -> 0 us
  other arithmetic: 70.3 us -> 45.3 us
  starting transfers between devices: 20.9 us -> 0.24 us
  local copies, waits for them, and re-layouts: 61.4 us -> 73.7 us
    psum x1, waiting for transfers between devices: 445 us -> 27.6 us  [body(): totals = lax.psum(shares, 'rep').astype(f32)]
    dot_general x30 -> x57, matrix products: 135 us -> 411 us  [the longest x4 65.9 us: gathered(): jnp.einsum('lmd,lmf->ldf', xg, d_gate, preferred_element_type=f32)]
    all_gather x4 -> x3, waiting for transfers between devices: 66.3 us -> 257 us  [the longest x1 124 us: body(): arrived = lax.all_gather(sent, axes, axis=0, tiled=True)]
    all_to_all x4 -> x0, waiting for transfers between devices: 144 us -> none  [the longest x1 53.2 us: body(): lax.all_to_all(grad_rows, 'shard', split_axis=0, concat_axis=0, tiled=True)]
    reduce_scatter x4 -> x2, waiting for transfers between devices: 106 us -> 0.01 us  [the longest x1 0.01 us: body(): lax.psum_scatter(back, 'shard', scatter_dimension=0, tiled=True).astype(f32)]
    all_gather x3 -> x0, blocking collectives: 93.5 us -> none  [the longest x1 74.6 us: gather_layer(): lax.all_gather(w_router, 'shard', axis=0, tiled=True)]
    transpose x0 -> x18, local copies, waits for them, and re-layouts: none -> 34.7 us  [the longest x4 15.4 us: gathered(): xg = jnp.einsum('blst,btd->lbsd', one_hot, rows).reshape(local, -1, width)]
    gather x2 -> x0, local copies, waits for them, and re-layouts: 29 us -> none  [the longest x1 14.5 us: body(): returned_rows.reshape(EXPERTS * CAP, MODEL_WIDTH)[state[14]]]
  transfers between devices with their start and end apart: 14 -> 6, of which waited for: 11 -> 4; matrix products, arithmetic and copies ran while one was open for 15% -> 31% of each run, Pallas kernels for 0% -> 0%
where the time goes in v1:
time: 844 us; the launch traced here: 835 us
  matrix products  415 us (49%)
  waiting for transfers between devices  285 us (34%)
  local copies, waits for them, and re-layouts  73.7 us (9%)
  other arithmetic  45.3 us (5%)
  between operations  16.3 us (2%)
    all_gather x1, waiting for transfers between devices, body(): arrived = lax.all_gather(sent, axes, axis=0, tiled=True)  124 us
    all_gather x1, waiting for transfers between devices, body(): all_cot = lax.all_gather(cotangent, axes, axis=0, tiled=True)  87.7 us
    dot_general x4, matrix products, gathered(): jnp.einsum('lmd,lmf->ldf', xg, d_gate, preferred_element_type=f32)  65.9 us
    dot_general x4, matrix products, gathered(): jnp.einsum('lmd,lmf->ldf', xg, d_up, preferred_element_type=f32)  59 us
    dot_general x4, matrix products, gathered(): jnp.einsum('lmf,lmd->lfd', scaled, cg, preferred_element_type=f32)  55.6 us
    all_gather x1, waiting for transfers between devices, body(): packed = lax.all_gather(packed, 'shard', axis=0, tiled=True)  45.2 us
    dot_general x4, matrix products, gathered(): raw = jnp.einsum('lmd,lfd->lmf', cg, w_down, preferred_element_type=f32)  39.8 us
    dot_general x4, matrix products, gathered(): up_part = jnp.einsum('lmd,ldf->lmf', xg, w_up, preferred_element_type=f32)  38.2 us
  transfers between devices with their start and end apart: 6, of which 4 were waited for; matrix products, arithmetic and copies ran while one was open for 31% of the time, Pallas kernels for 0%

profile of v1, /device:TPU:0, one launch (start us, length us, event | category | flops | bytes accessed | tf_op | source)
XLA Modules:
  0.0 835.5 jit_solution(13934311828291077232)
XLA Ops:
  17.2 45.2 %all-gather.4.cloned.1.call-done = bf16[1024,3200]{1,0:T(8,128)(2,1)} async-done(((bf16[128,3200]{1,0:T(8,128)(2,1)}), bf16[1024,3200]{1,0:T(8,128)(2,1)}) %all-gather.4.cloned.1.call-update) | async-done | bytes 6553616 | tf_op jit(solution)/shard_map/all_gather | solution.py:93
  85.2 124.0 %all-gather.6.cloned.1.call-done = bf16[8192,1152]{1,0:T(8,128)(2,1)} async-done(((bf16[256,1152]{1,0:T(8,128)(2,1)}), bf16[8192,1152]{1,0:T(8,128)(2,1)}) %all-gather.6.cloned.1.call-update) | async-done | bytes 18874384 | tf_op jit(solution)/shard_map/all_gather | solution.py:132
  218.9 13.0 %dynamic-slice_bitcast_fusion = (bf16[8,256,1152]{2,1,0:T(8,128)(2,1)}, bf16[8,256,1152]{2,1,0:T(8,128)(2,1)S(1)}, bf16[8,256,1152]{2,1,0:T(8,128)(2,1)}, bf16[8,256,1152]{2,1,0:T(8,128)(2,1)}) fusion(bf16[4,8,256,1152]{3,2,1,0:T(8,128)(2,1)} %bitcast.302, s32[]{:T(128)S(6)} %select_n.86, s32[]{:T(128)S(6)} %select_n.83, s32[]{:T(128)S(6)} %select_n.80, ...), kind=kLoop, calls=%fused_computation.37 | loop fusion | bytes 37748752 | tf_op jit(solution)/shard_map/jit(dynamic_index_in_dim)/squeeze | solution.py:139
  237.4 87.7 %all-gather.8.cloned.1.call-done = bf16[8192,1024]{1,0:T(8,128)(2,1)} async-done(((bf16[256,1024]{1,0:T(8,128)(2,1)}), bf16[8192,1024]{1,0:T(8,128)(2,1)}) %all-gather.8.cloned.1.call-update) | async-done | bytes 16777232 | tf_op jit(solution)/shard_map/all_gather | solution.py:101
  325.1 6.8 fusion.74
  331.9 6.8 fusion.79
  338.7 4.5 fusion.93
  347.3 5.5 fusion.242
  352.8 8.8 %fusion.239 = f32[4,768,512]{1,2,0:T(8,128)} fusion(bf16[4,768,1024]{2,1,0:T(8,128)(2,1)} %bitcast.319, bf16[4,1024,512]{2,1,0:T(8,128)(2,1)S(1)} %copy-done.9), kind=kOutput, calls=%fused_computation.296 | convolution fusion | flops 3221225472 | bytes 16777216 | tf_op jit(solution)/shard_map/lmd,ldf->lmf/dot_general | solution.py:148
  361.6 8.4 %fusion.241 = f32[4,768,512]{1,2,0:T(8,128)} fusion(bf16[4,768,1024]{2,1,0:T(8,128)(2,1)S(1)} %bitcast.308, bf16[4,1024,512]{2,1,0:T(8,128)(2,1)} %param.26), kind=kOutput, calls=%fused_computation.298 | convolution fusion | flops 3221225472 | bytes 16777216 | tf_op jit(solution)/shard_map/lmd,ldf->lmf/dot_general | solution.py:149
  370.0 10.2 %fusion.238 = f32[4,768,512]{1,2,0:T(8,128)} fusion(bf16[4,768,1024]{2,1,0:T(8,128)(2,1)} %bitcast.320, bf16[4,1024,512]{2,1,0:T(8,128)(2,1)} %param.26), kind=kOutput, calls=%fused_computation.295 | convolution fusion | flops 3221225472 | bytes 16777216 | tf_op jit(solution)/shard_map/lmd,ldf->lmf/dot_general | solution.py:149
  380.4 6.9 fusion.64
  387.3 4.5 fusion.84
  395.7 10.9 %fusion.230 = f32[4,768,512]{1,2,0:T(8,128)} fusion(bf16[4,768,1024]{2,1,0:T(8,128)(2,1)S(1)} %bitcast.295, bf16[4,1024,512]{2,1,0:T(8,128)(2,1)} %param.26), kind=kOutput, calls=%fused_computation.287 | convolution fusion | flops 3221225472 | bytes 16777216 | tf_op jit(solution)/shard_map/lmd,ldf->lmf/dot_general | solution.py:149
  406.6 5.4 fusion.229
  419.9 4.1 fusion.87
  438.3 15.0 %multiply_reduce_fusion = (f32[4,768]{1,0:T(4,128)S(1)}, f32[4,768,512]{1,2,0:T(8,128)}) fusion(f32[4,768,512]{1,2,0:T(8,128)} %fusion.230, f32[4,768,512]{1,2,0:T(8,128)} %fusion.229, bf16[4,768,1024]{2,1,0:T(8,128)(2,1)S(1)} %bitcast.299, bf16[4,512,1024]{2,1,0:T(8,128)(2,1)} %param.27), kind=kOutput, calls=%fused_computation.31 | convolution fusion | flops 3232232448 | bytes 29372416 | tf_op jit(solution)/shard_map/lmd,lfd->lmf/dot_general | solution.py:150
  456.7 8.4 %multiply_convert_fusion.11 = (bf16[4,768,512]{1,2,0:T(8,128)(2,1)S(1)}, bf16[4,768,512]{1,2,0:T(8,128)(2,1)S(1)}, bf16[4,768,512]{1,2,0:T(8,128)(2,1)S(1)}) fusion(f32[4,768]{1,0:T(4,128)S(1)} %mul.709, f32[4,768,512]{1,2,0:T(8,128)} %fusion.230, f32[4,768,512]{1,2,0:T(8,128)} %fusion.229, f32[4,768,512]{1,2,0:T(8,128)} %get-tuple-element.124), kind=kLoop, calls=%fused_computation.34 | loop fusion | flops 26738688 | bytes 28323840 | tf_op jit(solution)/shard_map/convert_element_type | solution.py:157
  465.1 5.6 convolution_convert_fusion.1
  470.7 7.3 bitcast_convert_fusion.1
  478.1 6.7 fusion.231
  484.8 9.6 %add_convert_fusion = bf16[4,768,1024]{2,1,0:T(8,128)(2,1)} fusion(f32[4,768,1024]{2,1,0:T(8,128)} %fusion.231, bf16[4,768,512]{1,2,0:T(8,128)(2,1)S(1)} %get-tuple-element.91, bf16[4,1024,512]{2,1,0:T(8,128)(2,1)} %param.26), kind=kOutput, calls=%fused_computation.4 | convolution fusion | flops 3227516928 | bytes 26214400 | tf_op jit(solution)/shard_map/lmf,ldf->lmd/dot_general | solution.py:168
  494.4 7.2 bitcast_convert_fusion
  503.5 7.1 pad_maximum_fusion
  510.8 4.2 fusion.69
  520.6 5.8 fusion.236
  526.4 8.7 %fusion.235 = f32[4,768,512]{1,2,0:T(8,128)} fusion(bf16[4,768,1024]{2,1,0:T(8,128)(2,1)S(1)} %bitcast.328, bf16[4,1024,512]{2,1,0:T(8,128)(2,1)} %param.26), kind=kOutput, calls=%fused_computation.292 | convolution fusion | flops 3221225472 | bytes 16777216 | tf_op jit(solution)/shard_map/lmd,ldf->lmf/dot_general | solution.py:149
  535.2 11.0 %fusion.234 = f32[4,768,512]{1,2,0:T(8,128)} fusion(bf16[4,768,1024]{2,1,0:T(8,128)(2,1)} %bitcast.329, bf16[4,512,1024]{2,1,0:T(8,128)(2,1)} %param.27), kind=kOutput, calls=%fused_computation.291 | convolution fusion | flops 3221225472 | bytes 16777216 | tf_op jit(solution)/shard_map/lmd,lfd->lmf/dot_general | solution.py:150
  546.2 8.4 %fusion.237 = f32[4,768,512]{1,2,0:T(8,128)} fusion(bf16[4,768,1024]{2,1,0:T(8,128)(2,1)} %bitcast.335, bf16[4,512,1024]{2,1,0:T(8,128)(2,1)S(1)} %copy-done.52), kind=kOutput, calls=%fused_computation.294 | convolution fusion | flops 3221225472 | bytes 16777216 | tf_op jit(solution)/shard_map/lmd,lfd->lmf/dot_general | solution.py:150
  554.6 5.5 fusion.240
  560.1 12.0 %fusion.39 = f32[4,512,1024]{2,1,0:T(8,128)} fusion(bf16[4,768,1024]{2,1,0:T(8,128)(2,1)S(1)} %bitcast.334, f32[4,768,512]{1,2,0:T(8,128)} %fusion.241, f32[4,768]{1,0:T(4,128)S(1)} %mul.780, f32[4,768,512]{1,2,0:T(8,128)} %fusion.242), kind=kOutput, calls=%fused_computation.79 | convolution fusion | flops 3232235520 | bytes 27275264 | tf_op jit(solution)/shard_map/lmf,lmd->lfd/dot_general | solution.py:161
  572.0 13.2 %fusion.38 = f32[4,512,1024]{2,1,0:T(8,128)} fusion(bf16[4,768,1024]{2,1,0:T(8,128)(2,1)} %bitcast.336, f32[4,768,512]{1,2,0:T(8,128)} %fusion.238, f32[4,768]{1,0:T(4,128)S(1)} %copy-done.45, f32[4,768,512]{1,2,0:T(8,128)} %fusion.239), kind=kOutput, calls=%fused_computation.78 | convolution fusion | flops 3232235520 | bytes 27275264 | tf_op jit(solution)/shard_map/lmf,lmd->lfd/dot_general | solution.py:161
  585.3 14.5 %fusion.35 = f32[4,1024,512]{2,1,0:T(8,128)} fusion(bf16[4,768,1024]{2,1,0:T(8,128)(2,1)} %bitcast.321, f32[4,768,512]{1,2,0:T(8,128)} %fusion.237, f32[4,768]{1,0:T(4,128)S(1)} %copy-done.45, f32[4,768,512]{1,2,0:T(8,128)} %fusion.239), kind=kOutput, calls=%fused_computation.75 | convolution fusion | flops 3232235520 | bytes 27275264 | tf_op jit(solution)/shard_map/lmd,lmf->ldf/dot_general | solution.py:160
  599.8 14.7 %fusion.36 = f32[4,1024,512]{2,1,0:T(8,128)} fusion(bf16[4,768,1024]{2,1,0:T(8,128)(2,1)} %bitcast.309, f32[4,768,512]{1,2,0:T(8,128)} %fusion.240, f32[4,768]{1,0:T(4,128)S(1)} %mul.780, f32[4,768,512]{1,2,0:T(8,128)} %fusion.242), kind=kOutput, calls=%fused_computation.76 | convolution fusion | flops 3232235520 | bytes 27275264 | tf_op jit(solution)/shard_map/lmd,lmf->ldf/dot_general | solution.py:160
  614.5 14.4 %fusion.34 = f32[4,1024,512]{2,1,0:T(8,128)} fusion(bf16[4,768,1024]{2,1,0:T(8,128)(2,1)} %bitcast.323, f32[4,768,512]{1,2,0:T(8,128)} %fusion.234, f32[4,768]{1,0:T(4,128)S(1)} %copy-done.43, f32[4,768,512]{1,2,0:T(8,128)} %fusion.236), kind=kOutput, calls=%fused_computation.74 | convolution fusion | flops 3232235520 | bytes 27275264 | tf_op jit(solution)/shard_map/lmd,lmf->ldf/dot_general | solution.py:160
  644.4 8.0 fusion.144
  652.4 8.2 fusion.111
  662.9 4.4 convolution_convert_fusion
  667.4 4.5 fusion.160
  672.1 5.6 fusion.3
  678.4 14.6 %fusion.37 = f32[4,512,1024]{2,1,0:T(8,128)} fusion(bf16[4,768,1024]{2,1,0:T(8,128)(2,1)} %bitcast.330, f32[4,768,512]{1,2,0:T(8,128)} %fusion.235, f32[4,768]{1,0:T(4,128)S(1)} %copy-done.44, f32[4,768,512]{1,2,0:T(8,128)} %fusion.236), kind=kOutput, calls=%fused_computation.77 | convolution fusion | flops 3232235520 | bytes 27275264 | tf_op jit(solution)/shard_map/lmf,lmd->lfd/dot_general | solution.py:161
  693.1 9.8 %fusion.233 = f32[4,1024,512]{2,1,0:T(8,128)} fusion(bf16[4,768,1024]{2,1,0:T(8,128)(2,1)} %bitcast.297, bf16[4,768,512]{1,2,0:T(8,128)(2,1)S(1)} %copy-done.6), kind=kOutput, calls=%fused_computation.290 | convolution fusion | flops 3221225472 | bytes 17825792 | tf_op jit(solution)/shard_map/lmd,lmf->ldf/dot_general | solution.py:159
  702.8 17.3 %fusion.47 = f32[4,1024,512]{2,1,0:T(8,128)} fusion(bf16[4,768,1024]{2,1,0:T(8,128)(2,1)} %bitcast.322, f32[4,768,512]{1,2,0:T(8,128)} %fusion.239, f32[4,768,512]{1,2,0:T(8,128)} %fusion.238, f32[4,768,512]{1,2,0:T(8,128)} %fusion.237, f32[4,768]{1,0:T(4,128)S(1)} %copy-done.46), kind=kOutput, calls=%fused_computation.96 | convolution fusion | flops 3238526976 | bytes 33566720 | tf_op jit(solution)/shard_map/lmd,lmf->ldf/dot_general | solution.py:159
  720.2 17.0 %fusion.46 = f32[4,1024,512]{2,1,0:T(8,128)} fusion(bf16[4,768,1024]{2,1,0:T(8,128)(2,1)} %bitcast.324, f32[4,768,512]{1,2,0:T(8,128)} %fusion.236, f32[4,768,512]{1,2,0:T(8,128)} %fusion.235, f32[4,768,512]{1,2,0:T(8,128)} %fusion.234, f32[4,768]{1,0:T(4,128)S(1)} %copy-done.44), kind=kOutput, calls=%fused_computation.95 | convolution fusion | flops 3238526976 | bytes 33566720 | tf_op jit(solution)/shard_map/lmd,lmf->ldf/dot_general | solution.py:159
  737.2 15.8 %add_add_fusion = f32[4,512,1024]{2,1,0:T(8,128)} fusion(f32[4,512,1024]{2,1,0:T(8,128)} %fusion.39, f32[4,512,1024]{2,1,0:T(8,128)} %fusion.38, f32[4,512,1024]{2,1,0:T(8,128)} %fusion.37, bf16[4,768,512]{1,2,0:T(8,128)(2,1)S(1)} %copy-done.8, bf16[4,768,1024]{2,1,0:T(8,128)(2,1)} %bitcast.300), kind=kOutput, calls=%fused_computation.8 | convolution fusion | flops 3227516928 | bytes 42991616 | tf_op jit(solution)/shard_map/lmf,lmd->lfd/dot_general | solution.py:161
  753.0 21.8 %add_add_fusion.2 = f32[4,1024,512]{2,1,0:T(8,128)} fusion(f32[4,1024,512]{2,1,0:T(8,128)} %fusion.47, f32[4,1024,512]{2,1,0:T(8,128)} %fusion.233, f32[4,1024,512]{2,1,0:T(8,128)} %fusion.46, bf16[4,768,1024]{2,1,0:T(8,128)(2,1)} %bitcast.310, f32[4,768,512]{1,2,0:T(8,128)} %fusion.242, f32[4,768,512]{1,2,0:T(8,128)} %fusion.241, ...), kind=kOutput, calls=%fused_computation.10 | convolution fusion | flops 3244818432 | bytes 58732544 | tf_op jit(solution)/shard_map/lmd,lmf->ldf/dot_general | solution.py:159
  774.8 15.5 %add_add_fusion.1 = f32[4,1024,512]{2,1,0:T(8,128)} fusion(f32[4,1024,512]{2,1,0:T(8,128)} %fusion.36, f32[4,1024,512]{2,1,0:T(8,128)} %fusion.35, f32[4,1024,512]{2,1,0:T(8,128)} %fusion.34, bf16[4,768,1024]{2,1,0:T(8,128)(2,1)} %bitcast.298, bf16[4,768,512]{1,2,0:T(8,128)(2,1)S(1)} %copy-done.3), kind=kOutput, calls=%fused_computation.9 | convolution fusion | flops 3227516928 | bytes 42991616 | tf_op jit(solution)/shard_map/lmd,lmf->ldf/dot_general | solution.py:160
  793.3 27.6 %all-reduce.4.cloned.1.call-done = bf16[128,3200]{1,0:T(8,128)(2,1)} async-done(((bf16[128,3200]{1,0:T(8,128)(2,1)}), bf16[128,3200]{1,0:T(8,128)(2,1)}) %all-reduce.4.cloned.1.call-update) | async-done | bytes 819216 | tf_op jit(solution)/shard_map/psum | solution.py:219
  (275 shorter events, 117.0 us)
Async XLA Ops:
  7.2 58.7 %copy-start.19 = (bf16[256,1024]{1,0:T(8,128)(2,1)S(1)}, bf16[256,1024]{1,0:T(8,128)(2,1)}, u32[]{:S(2)}) copy-start(bf16[256,1024]{1,0:T(8,128)(2,1)} %param.14) | copy-start | bytes 1572868
  7.2 55.2 %all-gather.4.cloned.1.call-start = ((), (), s32[]{:S(2)}) async-start(), calls=%async_computation.2 | async-start | bytes 7372800 | tf_op jit(solution)/shard_map/all_gather | solution.py:93
  12.9 196.3 %all-gather.6.cloned.1.call-start = ((), (), s32[]{:S(2)}) async-start(), calls=%async_computation.3 | async-start | bytes 19464192 | tf_op jit(solution)/shard_map/all_gather | solution.py:132
  16.3 54.5 %copy-start.48 = (f32[256]{0:T(256)}, f32[256]{0:T(256)S(1)}, u32[]{:S(2)}) copy-start(f32[256]{0:T(256)S(1)} %get-tuple-element.111) | copy-start | bytes 3076
  17.2 53.5 %copy-start.25 = (f32[256,32]{0,1:T(8,128)}, f32[256,32]{0,1:T(8,128)S(1)}, u32[]{:S(2)}) copy-start(f32[256,32]{0,1:T(8,128)S(1)} %get-tuple-element.116) | copy-start | bytes 98308
  63.8 16.5 %copy-start.37 = (f32[1024]{0:T(1024)}, f32[1024]{0:T(1024)S(1)}, u32[]{:S(2)}) copy-start(f32[1024]{0:T(1024)S(1)} %get-tuple-element.72) | copy-start | bytes 12292
  65.8 8.4 %copy-start.23 = (bf16[256,512]{0,1:T(8,128)(2,1)}, bf16[256,512]{0,1:T(8,128)(2,1)S(1)}, u32[]{:S(2)}) copy-start(bf16[256,512]{0,1:T(8,128)(2,1)S(1)} %copy.360) | copy-start | bytes 786436
  80.3 128.9 %copy-start.41 = (f32[256]{0:T(256)}, f32[256]{0:T(256)S(1)}, u32[]{:S(2)}) copy-start(f32[256]{0:T(256)S(1)} %get-tuple-element.113) | copy-start | bytes 3076
  80.8 134.1 %copy-start.15 = (bf16[256,1024]{1,0:T(8,128)(2,1)}, bf16[256,1024]{1,0:T(8,128)(2,1)S(1)}, u32[]{:S(2)}) copy-start(bf16[256,1024]{1,0:T(8,128)(2,1)S(1)} %multiply_convert_fusion.24) | copy-start | bytes 1572868
  84.3 240.8 %all-gather.8.cloned.1.call-start = ((), (), s32[]{:S(2)}) async-start(), calls=%async_computation.4 | async-start | bytes 17301504 | tf_op jit(solution)/shard_map/all_gather | solution.py:101
  85.1 543.8 %reduce-scatter.3.cloned.1.call-start = ((), (), s32[]{:S(2)}) async-start(), calls=%async_computation.5 | async-start | bytes 10027008 | tf_op jit(solution)/shard_map/reduce_scatter | solution.py:179
  325.1 13.6 %slice-start.10 = ((s8[4718592]{0:T(1024)(128)(4,1)}), s8[4194304]{0:T(1024)(128)(4,1)S(1)}, s32[]{:S(2)}) async-start(s8[4718592]{0:T(1024)(128)(4,1)} %bitcast.340), calls=%async_computation.18 | async-start | bytes 8388608
  347.3 14.3 %copy-start.4 = (bf16[4,8,96,1024]{3,2,1,0:T(8,128)(2,1)}, bf16[4,8,96,1024]{3,2,1,0:T(8,128)(2,1)S(1)}, u32[]{:S(2)}) copy-start(bf16[4,8,96,1024]{3,2,1,0:T(8,128)(2,1)S(1)} %copy.419) | copy-start | bytes 18874372
  380.2 7.1 slice-start.8
  395.7 10.9 %copy-start = (bf16[4,8,96,1024]{3,2,1,0:T(8,128)(2,1)}, bf16[4,8,96,1024]{3,2,1,0:T(8,128)(2,1)S(1)}, u32[]{:S(2)}) copy-start(bf16[4,8,96,1024]{3,2,1,0:T(8,128)(2,1)S(1)} %copy.369) | copy-start | bytes 18874372
  419.9 8.1 slice-start.2
  424.1 7.3 slice-start
  438.3 15.0 %copy-start.1 = (bf16[4,8,96,1024]{3,2,1,0:T(8,128)(2,1)}, bf16[4,8,96,1024]{3,2,1,0:T(8,128)(2,1)S(1)}, u32[]{:S(2)}) copy-start(bf16[4,8,96,1024]{3,2,1,0:T(8,128)(2,1)S(1)} %copy.376) | copy-start | bytes 18874372
  456.7 8.5 %copy-start.51 = (bf16[4,512,1024]{2,1,0:T(8,128)(2,1)S(1)}, bf16[4,512,1024]{2,1,0:T(8,128)(2,1)}, u32[]{:S(2)}) copy-start(bf16[4,512,1024]{2,1,0:T(8,128)(2,1)} %param.27) | copy-start | bytes 12582916
  465.1 13.0 %copy-start.5 = (bf16[4,768,512]{1,2,0:T(8,128)(2,1)}, bf16[4,768,512]{1,2,0:T(8,128)(2,1)S(1)}, u32[]{:S(2)}) copy-start(bf16[4,768,512]{1,2,0:T(8,128)(2,1)S(1)} %get-tuple-element.90) | copy-start | bytes 9437188
  465.1 19.7 %copy-start.2 = (bf16[4,768,512]{1,2,0:T(8,128)(2,1)}, bf16[4,768,512]{1,2,0:T(8,128)(2,1)S(1)}, u32[]{:S(2)}) copy-start(bf16[4,768,512]{1,2,0:T(8,128)(2,1)S(1)} %get-tuple-element.91) | copy-start | bytes 9437188
  470.7 7.3 copy-start.10
  494.4 7.3 copy-start.18
  510.7 264.1 %reduce-scatter.5.cloned.1.call-start = ((), (), s32[]{:S(2)}) async-start(), calls=%async_computation.6 | async-start | bytes 7372800 | tf_op jit(solution)/shard_map/reduce_scatter | solution.py:218
  510.8 8.3 slice-start.4
  535.2 11.0 %copy-start.52 = (bf16[4,512,1024]{2,1,0:T(8,128)(2,1)S(1)}, bf16[4,512,1024]{2,1,0:T(8,128)(2,1)}, u32[]{:S(2)}) copy-start(bf16[4,512,1024]{2,1,0:T(8,128)(2,1)} %param.27) | copy-start | bytes 12582916
  535.2 19.4 %slice-start.6 = ((s8[6291456]{0:T(1024)(128)(4,1)}), s8[4194304]{0:T(1024)(128)(4,1)S(1)}, s32[]{:S(2)}) async-start(s8[6291456]{0:T(1024)(128)(4,1)} %bitcast.331), calls=%async_computation.14 | async-start | bytes 8388608
  546.2 8.4 %slice-start.7 = ((s8[6291456]{0:T(1024)(128)(4,1)}), s8[2097152]{0:T(1024)(128)(4,1)S(1)}, s32[]{:S(2)}) async-start(s8[6291456]{0:T(1024)(128)(4,1)} %bitcast.331), calls=%async_computation.15 | async-start | bytes 4194304
  560.1 12.0 %copy-start.45 = (f32[4,768]{1,0:T(4,128)S(1)}, f32[4,768]{1,0:T(4,128)}, u32[]{:S(2)}) copy-start(f32[4,768]{1,0:T(4,128)} %mul.771) | copy-start | bytes 36868
  599.8 14.7 %copy-start.43 = (f32[4,768]{1,0:T(4,128)S(1)}, f32[4,768]{1,0:T(4,128)}, u32[]{:S(2)}) copy-start(f32[4,768]{1,0:T(4,128)} %mul.762) | copy-start | bytes 36868
  614.5 15.9 %copy-start.22 = (f32[256,32]{1,0:T(8,128)S(1)}, f32[256,32]{1,0:T(8,128)}, u32[]{:S(2)}) copy-start(f32[256,32]{1,0:T(8,128)} %get-tuple-element.84) | copy-start | bytes 98308
  614.5 16.2 %copy-start.16 = (bf16[256,1024]{1,0:T(8,128)(2,1)S(1)}, bf16[256,1024]{1,0:T(8,128)(2,1)}, u32[]{:S(2)}) copy-start(bf16[256,1024]{1,0:T(8,128)(2,1)} %copy-done.15) | copy-start | bytes 1572868
  614.5 16.4 %copy-start.14 = (f32[256,1024]{1,0:T(8,128)S(1)}, f32[256,1024]{1,0:T(8,128)}, u32[]{:S(2)}) copy-start(f32[256,1024]{1,0:T(8,128)} %copy-done.13) | copy-start | bytes 3145732
  614.5 16.4 %copy-start.38 = (f32[1024]{0:T(1024)S(1)}, f32[1024]{0:T(1024)}, u32[]{:S(2)}) copy-start(f32[1024]{0:T(1024)} %copy-done.37) | copy-start | bytes 12292
  614.5 16.4 %copy-start.42 = (f32[256]{0:T(256)S(1)}, f32[256]{0:T(256)}, u32[]{:S(2)}) copy-start(f32[256]{0:T(256)} %copy-done.41) | copy-start | bytes 3076
  644.4 8.0 copy-start.34
  644.4 8.0 copy-start.36
  652.4 9.0 %copy-start.26 = (f32[256,32]{0,1:T(8,128)S(1)}, f32[256,32]{0,1:T(8,128)}, u32[]{:S(2)}) copy-start(f32[256,32]{0,1:T(8,128)} %copy-done.25) | copy-start | bytes 98308
  652.4 9.0 %copy-start.31 = (f32[256,8,64]{0,2,1:T(8,128)S(1)}, f32[256,8,64]{0,2,1:T(8,128)}, u32[]{:S(2)}) copy-start(f32[256,8,64]{0,2,1:T(8,128)} %fusion.144) | copy-start | bytes 1572868
  652.4 9.0 %copy-start.32 = (f32[256,32]{0,1:T(8,128)S(1)}, f32[256,32]{0,1:T(8,128)}, u32[]{:S(2)}) copy-start(f32[256,32]{0,1:T(8,128)} %get-tuple-element.114) | copy-start | bytes 98308
  652.4 10.5 %copy-start.20 = (bf16[256,1024]{1,0:T(8,128)(2,1)S(1)}, bf16[256,1024]{1,0:T(8,128)(2,1)}, u32[]{:S(2)}) copy-start(bf16[256,1024]{1,0:T(8,128)(2,1)} %param.14) | copy-start | bytes 1572868
  652.4 10.5 %copy-start.40 = (f32[1024]{0:T(1024)S(1)}, f32[1024]{0:T(1024)}, u32[]{:S(2)}) copy-start(f32[1024]{0:T(1024)} %copy-done.39) | copy-start | bytes 12292
  677.7 15.3 %copy-start.6 = (bf16[4,768,512]{1,2,0:T(8,128)(2,1)S(1)}, bf16[4,768,512]{1,2,0:T(8,128)(2,1)}, u32[]{:S(2)}) copy-start(bf16[4,768,512]{1,2,0:T(8,128)(2,1)} %copy-done.5) | copy-start | bytes 9437188
  677.8 143.1 %all-reduce.4.cloned.1.call-start = ((), (), s32[]{:S(2)}) async-start(), calls=%async_computation.7 | async-start | bytes 1638400 | tf_op jit(solution)/shard_map/psum | solution.py:219
  693.1 9.8 %copy-start.46 = (f32[4,768]{1,0:T(4,128)S(1)}, f32[4,768]{1,0:T(4,128)}, u32[]{:S(2)}) copy-start(f32[4,768]{1,0:T(4,128)} %mul.771) | copy-start | bytes 36868
  720.2 17.0 %copy-start.8 = (bf16[4,768,512]{1,2,0:T(8,128)(2,1)S(1)}, bf16[4,768,512]{1,2,0:T(8,128)(2,1)}, u32[]{:S(2)}) copy-start(bf16[4,768,512]{1,2,0:T(8,128)(2,1)} %copy-done.7) | copy-start | bytes 9437188
  753.0 21.8 %copy-start.3 = (bf16[4,768,512]{1,2,0:T(8,128)(2,1)S(1)}, bf16[4,768,512]{1,2,0:T(8,128)(2,1)}, u32[]{:S(2)}) copy-start(bf16[4,768,512]{1,2,0:T(8,128)(2,1)} %copy-done.2) | copy-start | bytes 9437188
  774.8 15.5 %copy-start.47 = (f32[256]{0:T(256)S(1)}, f32[256]{0:T(256)}, u32[]{:S(2)}) copy-start(f32[256]{0:T(256)} %get-tuple-element.110) | copy-start | bytes 3076
  (26 other events, 119.8 us)
Sparse Core Ops, SparseCore 0:
  13.0 49.3 all-gather.3
  84.5 124.6 all-gather.5
  212.0 113.0 all-gather.7
  510.8 74.1 reduce-scatter.2
  677.9 63.5 reduce-scatter.4
  774.9 45.9 all-reduce.3

commit v2 on v1

v2 whole, which is shorter than its diff:
```python
import functools
import math

import jax
import jax.numpy as jnp
from jax import lax
from jax.experimental import pallas as pl
from jax.experimental.pallas import tpu as pltpu
from jax.sharding import PartitionSpec as P

QUERY_HEADS = 16
KEY_VALUE_HEADS = 8
HEAD_SIZE = 64
CAP = 96
LANES = 128
MOST_GATHERED = 4

epsilon = 1e-06
score_scale = 0.015625
branch_scale = 0.22
masked_value = -1e30

f32 = jnp.float32
bf16 = jnp.bfloat16
MESH = pl.DeviceIdType.MESH


def dot(left, right, contract=((1,), (0,))):
    return lax.dot_general(left, right, (contract, ((), ())), preferred_element_type=f32)

def slot_ranks(gates):
    tokens = gates.shape[1]
    named = gates > 0
    before = lax.broadcasted_iota(jnp.int32, (tokens, tokens), 0) < lax.broadcasted_iota(jnp.int32, (tokens, tokens), 1)
    rank = dot(named.astype(f32).astype(bf16), before.astype(f32).astype(bf16))
    return jnp.where(named, rank, -1.0)

def pick_row(table, row):
    here = lax.broadcasted_iota(jnp.int32, table.shape, 0) == row
    return jnp.sum(jnp.where(here, table, 0.0), axis=0, keepdims=True)

def slot_one_hot(ranks, first, local):
    tokens = ranks.shape[1]
    slot = lax.broadcasted_iota(jnp.int32, (CAP, tokens), 0).astype(f32)
    return [jnp.where(pick_row(ranks, first + l) == slot, 1.0, 0.0) for l in range(local)]

def gather_block(x, c, gates, first, local, xg_ref, cg_ref, sg_ref, at):
    ranks = slot_ranks(gates)
    parts = slot_one_hot(ranks, first, local)
    table = jnp.concatenate(parts, axis=0).astype(bf16)
    xg = dot(table, x).astype(bf16)
    cg = dot(table, c).astype(bf16)
    for l in range(local):
        rows = slice(l * CAP, (l + 1) * CAP)
        xg_ref[l, pl.ds(at, CAP), :] = xg[rows]
        cg_ref[l, pl.ds(at, CAP), :] = cg[rows]
        gate = jnp.sum(parts[l] * pick_row(gates, first + l), axis=1, keepdims=True)
        sg_ref[l, pl.ds(at, CAP), :] = branch_scale * gate
    return parts

def expert_parts(xg, cg, scale, wg, wu, wd):
    gate_part = dot(xg, wg)
    up_part = dot(xg, wu)
    raw = dot(cg, wd, ((1,), (1,)))
    sigma = 1.0 / (1.0 + jnp.exp(-gate_part))
    act = gate_part * sigma
    inner = act * up_part
    d_inner = raw * scale
    d_gate = (d_inner * up_part * (sigma + act * (1.0 - sigma))).astype(bf16)
    d_up = (d_inner * act).astype(bf16)
    scaled = (inner * scale).astype(bf16)
    return inner, raw, d_gate, d_up, scaled

def sums_kernel(nb, x_hbm, c_hbm, g_ref, wg_hbm, wu_hbm, wd_hbm, og_hbm, ou_hbm, od_hbm,
                xbuf, cbuf, wg, wu, wd, ag, au, ad, xg_ref, cg_ref, sg_ref, sem, wsem):
    local = wg.shape[0]
    blocks = x_hbm.shape[0]
    chunks = blocks // nb
    first = lax.axis_index("shard") * local
    def fetch(i, slot):
        return (pltpu.make_async_copy(x_hbm.at[pl.ds(i * nb, nb)], xbuf.at[slot], sem.at[0, slot]),
                pltpu.make_async_copy(c_hbm.at[pl.ds(i * nb, nb)], cbuf.at[slot], sem.at[1, slot]))
    for cp in fetch(0, 0):
        cp.start()
    weights = [pltpu.make_async_copy(a, b, wsem.at[i]) for i, (a, b) in enumerate(((wg_hbm, wg), (wu_hbm, wu), (wd_hbm, wd)))]
    for cp in weights:
        cp.start()
    ag[...] = jnp.zeros_like(ag)
    au[...] = jnp.zeros_like(au)
    ad[...] = jnp.zeros_like(ad)
    for cp in weights:
        cp.wait()

    def chunk(i, carry):
        slot = lax.rem(i, 2)
        @pl.when(i + 1 < chunks)
        def _():
            for cp in fetch(i + 1, 1 - slot):
                cp.start()
        for cp in fetch(i, slot):
            cp.wait()
        def block(b, carry):
            gather_block(xbuf[slot, b], cbuf[slot, b], g_ref[i * nb + b], first, local, xg_ref, cg_ref, sg_ref,
                         pl.multiple_of(b * CAP, CAP))
            return carry
        lax.fori_loop(0, nb, block, 0)
        def expert(l, carry):
            xg, cg = xg_ref[l], cg_ref[l]
            _, _, d_gate, d_up, scaled = expert_parts(xg, cg, sg_ref[l], wg[l], wu[l], wd[l])
            ag[l] += dot(xg, d_gate, ((0,), (0,)))
            au[l] += dot(xg, d_up, ((0,), (0,)))
            ad[l] += dot(scaled, cg, ((0,), (0,)))
            return carry
        lax.fori_loop(0, local, expert, 0)
        return carry
    lax.fori_loop(0, chunks, chunk, 0)
    outs = [pltpu.make_async_copy(a, b, wsem.at[i]) for i, (a, b) in enumerate(((ag, og_hbm), (au, ou_hbm), (ad, od_hbm)))]
    for cp in outs:
        cp.start()
    for cp in outs:
        cp.wait()

def moe_sums(x, c, gates, wg, wu, wd, nb=4):
    _, tokens, width = x.shape
    local, _, hidden = wg.shape
    any_ = pl.BlockSpec(memory_space=pl.ANY)
    rows = nb * CAP
    return pl.pallas_call(
        functools.partial(sums_kernel, nb),
        out_shape=[jax.ShapeDtypeStruct(w.shape, f32) for w in (wg, wu, wd)],
        in_specs=[any_, any_, pl.BlockSpec(memory_space=pltpu.VMEM), any_, any_, any_],
        out_specs=[any_] * 3,
        scratch_shapes=[
            pltpu.VMEM((2, nb, tokens, width), bf16), pltpu.VMEM((2, nb, tokens, width), bf16),
            pltpu.VMEM(wg.shape, bf16), pltpu.VMEM(wu.shape, bf16), pltpu.VMEM(wd.shape, bf16),
            pltpu.VMEM(wg.shape, f32), pltpu.VMEM(wu.shape, f32), pltpu.VMEM(wd.shape, f32),
            pltpu.VMEM((local, rows, width), bf16), pltpu.VMEM((local, rows, width), bf16), pltpu.VMEM((local, rows, 1), f32),
            pltpu.SemaphoreType.DMA((2, 2)), pltpu.SemaphoreType.DMA((3,)),
        ],
        compiler_params=pltpu.CompilerParams(vmem_limit_bytes=60 << 20),
        name="expert_sums",
    )(x, c, gates, wg, wu, wd)


def norm_scale(rows):
    return lax.rsqrt(jnp.mean(rows * rows, axis=-1, keepdims=True) + epsilon)

def flip(index, bit):
    return index + bit - 2 * bit * ((index // bit) % 2)

def turned(index, core, step, bits):
    return (1 - core) * flip(index, bits[step]) + core * flip(index, bits[-1 - step])

class PlaneGather:
    def __init__(self, buf, send, recv, base=0):
        self.buf, self.send, self.recv, self.base = buf, send, recv, base
        self.rep, self.me = lax.axis_index("rep"), lax.axis_index("shard")
        self.core = self.me % 2
        shards = lax.axis_size("shard")
        self.bits = [1 << i for i in range(1, shards.bit_length() - 1)]
        self.steps = len(self.bits)

    @staticmethod
    def copies(shards):
        return (shards // 2 - 1) + shards // 2

    def owner(self, of, subset):
        for step in range(self.steps):
            if subset >> step & 1:
                of = turned(of, self.core, step, self.bits)
        return of

    def copy(self, number, owner, target):
        return pltpu.make_async_remote_copy(
            src_ref=self.buf.at[owner], dst_ref=self.buf.at[owner],
            send_sem=self.send.at[self.base + number], recv_sem=self.recv.at[self.base + number],
            device_id=(self.rep, target), device_id_type=MESH,
        )

    def chip_copy(self, step, subset):
        return self.copy((1 << step) - 1 + subset, self.owner(self.me, subset), turned(self.me, self.core, step, self.bits))

    def core_copy(self, subset):
        return self.copy((1 << self.steps) - 1 + subset, self.owner(self.me, subset), flip(self.me, 1))

    def start(self):
        for step in range(self.steps):
            self.chip_copy(step, 0).start()
        self.core_copy(0).start()

    def forward(self, step):
        for subset in range(1 << step):
            self.chip_copy(step, subset).wait_recv()
            whole = subset + (1 << step)
            for later in range(step + 1, self.steps):
                self.chip_copy(later, whole).start()
            self.core_copy(whole).start()

    def finish(self):
        for subset in range(1 << self.steps):
            self.core_copy(subset).wait_recv()
        for step in range(self.steps):
            for subset in range(1 << step):
                self.chip_copy(step, subset).wait_send()
        for subset in range(1 << self.steps):
            self.core_copy(subset).wait_send()

def rotate(v, cosine, sine, sign):
    lane = lax.broadcasted_iota(jnp.int32, v.shape, 1) % HEAD_SIZE
    half = HEAD_SIZE // 2
    low = lane < half
    other = jnp.where(low, -pltpu.roll(v, LANES - half, 1), pltpu.roll(v, half, 1))
    return v * cosine + sign * other * sine

def two_heads(v):
    low = lax.broadcasted_iota(jnp.int32, v.shape, 1) < HEAD_SIZE
    zero = jnp.zeros_like(v)
    return jnp.concatenate([jnp.where(low, v, zero), jnp.where(low, zero, v)], axis=0)

def one_head_twice(pair, odd):
    high = lax.broadcasted_iota(jnp.int32, pair.shape, 1) // HEAD_SIZE
    wide = pair.astype(f32)
    return jnp.where(high == odd, wide, pltpu.roll(wide, HEAD_SIZE, 1)).astype(pair.dtype)

def probabilities(query2, keys, prefix_len):
    rows = query2.shape[0] // 2
    raw = dot(query2, keys, ((1,), (1,)))
    row = lax.broadcasted_iota(jnp.int32, raw.shape, 0) % rows
    col = lax.broadcasted_iota(jnp.int32, raw.shape, 1)
    scores = jnp.where((col <= row) | (col < prefix_len), raw * score_scale, masked_value)
    weights = jnp.exp(scores - jnp.max(scores, axis=-1, keepdims=True))
    return weights / jnp.sum(weights, axis=-1, keepdims=True)

def lanes(j, count=1):
    return pl.ds(pl.multiple_of(j * LANES * count, LANES), LANES * count)

def front_kernel(prefix_ref, tok_ref, routes_ref, cos_ref, sin_ref, mine_ref,
                 wall_out, q_out, k_out, v_out, att_out, hid_out, x_out, gates_out, n1_out,
                 wbuf, qkv_ref, send, recv, lsem):
    count, width = tok_ref.shape
    kv_width = k_out.shape[1]
    experts = gates_out.shape[0]
    shards, depth, total = wbuf.shape
    me = lax.axis_index("shard")
    own = pltpu.make_async_copy(mine_ref, wbuf.at[me], lsem.at[0])
    own.start()
    gather = PlaneGather(wbuf, send, recv)
    own.wait()
    gather.start()
    inputs = tok_ref[...].astype(f32)
    scaled = inputs * norm_scale(inputs)
    for step in range(gather.steps):
        gather.forward(step)
    gather.finish()
    keep = pltpu.make_async_copy(wbuf, wall_out, lsem.at[1])
    keep.start()
    cut = [0, width, width + kv_width, width + 2 * kv_width, 2 * width + 2 * kv_width]
    small = wbuf[:, :, cut[4]:].reshape(shards * depth, total - cut[4])
    wide = small.astype(f32).T
    gain_one, gain_two = wide[experts:experts + 1], wide[experts + 1:experts + 2]
    n1_out[...] = (scaled * gain_one).astype(bf16)

    def project(j, carry):
        w = wbuf[:, :, lanes(j, 2)].reshape(shards * depth, 2 * LANES)
        qkv_ref[:, lanes(j, 2)] = dot(n1_out[...], w)
        return carry
    lax.fori_loop(0, cut[3] // (2 * LANES), project, 0)
    cosine, sine = cos_ref[...], sin_ref[...]
    for j in range(width // LANES):
        q_out[:, j * LANES:(j + 1) * LANES] = rotate(qkv_ref[:, j * LANES:(j + 1) * LANES], cosine, sine, 1.0).astype(bf16)
    for j in range(kv_width // LANES):
        at = slice(cut[1] + j * LANES, cut[1] + (j + 1) * LANES)
        k_out[:, j * LANES:(j + 1) * LANES] = rotate(qkv_ref[:, at], cosine, sine, 1.0).astype(bf16)
    v_out[...] = qkv_ref[:, cut[2]:cut[3]].astype(bf16)
    prefix_len = prefix_ref[0]

    def head(j, carry):
        keys = one_head_twice(k_out[:, lanes(j // 2)], j % 2)
        values = one_head_twice(v_out[:, lanes(j // 2)], j % 2)
        prob = probabilities(two_heads(q_out[:, lanes(j)]), keys, prefix_len)
        both = dot(prob.astype(bf16), values)
        low = lax.broadcasted_iota(jnp.int32, (count, LANES), 1) < HEAD_SIZE
        att_out[:, lanes(j)] = jnp.where(low, both[:count], both[count:]).astype(bf16)
        return carry
    lax.fori_loop(0, KEY_VALUE_HEADS, head, 0)

    def project_out(j, carry):
        w = wbuf[:, :, pl.ds(pl.multiple_of(cut[3] + j * 2 * LANES, LANES), 2 * LANES)].reshape(shards * depth, 2 * LANES)
        qkv_ref[:, lanes(j, 2)] = dot(att_out[...], w)
        return carry
    lax.fori_loop(0, width // (2 * LANES), project_out, 0)
    hidden = inputs + branch_scale * qkv_ref[:, :width]
    hid_out[...] = hidden
    x = (hidden * norm_scale(hidden) * gain_two).astype(bf16)
    x_out[...] = x
    logits = dot(x, small).T[:experts]
    expert = lax.broadcasted_iota(jnp.int32, (experts, count), 0)
    named = expert < 0
    for k in range(routes_ref.shape[0]):
        named = named | (routes_ref[k:k + 1, :] == expert)
    top = jnp.max(jnp.where(named, logits, masked_value), axis=0, keepdims=True)
    weights = jnp.where(named, jnp.exp(jnp.where(named, logits - top, 0.0)), 0.0)
    gates_out[...] = weights / jnp.sum(weights, axis=0, keepdims=True)
    keep.wait()

def front(tokens, prefix, routes, mine, cosine, sine, experts, kv_width):
    count, width = tokens.shape
    shards = lax.axis_size("shard")
    depth, total = mine.shape
    v = pl.BlockSpec(memory_space=pltpu.VMEM)
    any_ = pl.BlockSpec(memory_space=pl.ANY)
    sds = jax.ShapeDtypeStruct
    n = PlaneGather.copies(shards)
    return pl.pallas_call(
        front_kernel,
        out_shape=[
            sds((shards, depth, total), bf16), sds((count, width), bf16), sds((count, kv_width), bf16), sds((count, kv_width), bf16),
            sds((count, width), bf16), sds((count, width), f32), sds((count, width), bf16), sds((experts, count), f32), sds((count, width), bf16),
        ],
        in_specs=[pl.BlockSpec(memory_space=pltpu.SMEM), v, v, v, v, any_],
        out_specs=[any_] + [v] * 8,
        scratch_shapes=[
            pltpu.VMEM((shards, depth, total), bf16), pltpu.VMEM((count, width + 2 * kv_width), f32),
            pltpu.SemaphoreType.DMA((n,)), pltpu.SemaphoreType.DMA((n,)), pltpu.SemaphoreType.DMA((2,)),
        ],
        compiler_params=pltpu.CompilerParams(vmem_limit_bytes=60 << 20, has_side_effects=True),
        name="front",
    )(prefix, tokens, routes, cosine, sine, mine)

def rotary_tables(count):
    half = HEAD_SIZE // 2
    places = jnp.arange(count, dtype=f32)
    inverse = jnp.exp(jnp.arange(half, dtype=f32) * (-2.0 * math.log(10000.0) / HEAD_SIZE))
    angles = jnp.tile(places[:, None] * inverse[None, :], (1, LANES // half))
    return jnp.cos(angles), jnp.sin(angles)


def pack(w_query, key_weight, value_weight, w_out, w_router, norm_attn, norm_moe):
    small = jnp.concatenate([w_router, norm_attn[:, None], norm_moe[:, None]], axis=1)
    small = jnp.pad(small, ((0, 0), (0, LANES - small.shape[1])))
    return jnp.concatenate([w_query, key_weight, value_weight, w_out, small], axis=1)


def norm_backward(rows, scaling, gain, upstream):
    weighted = upstream * gain
    inner_mean = jnp.mean(weighted * rows, axis=-1, keepdims=True)
    gradient = scaling * weighted - rows * (scaling * scaling * scaling) * inner_mean
    return gradient, jnp.sum(upstream * rows * scaling, axis=0, keepdims=True)


def turn_back(rows, cosine, sine):
    count = rows.shape[0]
    half = HEAD_SIZE // 2
    shaped = rows.reshape(count, -1, HEAD_SIZE)
    first, second = shaped[..., :half], shaped[..., half:]
    c, s = cosine[:, None, :half], sine[:, None, :half]
    return jnp.concatenate([first * c + second * s, second * c - first * s], axis=-1).reshape(rows.shape)


def own_part(x, c, gates, first, w_gate, w_up, w_down):
    local, width, hidden = w_gate.shape
    shards, count, _ = x.shape
    mine = lax.dynamic_slice_in_dim(gates, first, local, axis=1)
    named = mine > 0
    place = jnp.arange(count)
    earlier = (place[:, None] < place[None, :]).astype(bf16)
    rank = jnp.einsum("bls,st->blt", named.astype(bf16), earlier, preferred_element_type=f32)
    here = (rank[:, :, None, :] == jnp.arange(CAP, dtype=f32)[None, None, :, None]) & named[:, :, None, :]
    one_hot = here.astype(bf16)
    slot_gate = jnp.sum(jnp.where(here, mine[:, :, None, :], 0.0), axis=3)
    xg = jnp.einsum("blst,btd->lbsd", one_hot, x).reshape(local, -1, width)
    cg = jnp.einsum("blst,btd->lbsd", one_hot, c).reshape(local, -1, width)
    scale = branch_scale * slot_gate.transpose(1, 0, 2).reshape(local, -1)[:, :, None]
    gate_part = jnp.einsum("lmd,ldf->lmf", xg, w_gate, preferred_element_type=f32)
    up_part = jnp.einsum("lmd,ldf->lmf", xg, w_up, preferred_element_type=f32)
    raw = jnp.einsum("lmd,lfd->lmf", cg, w_down, preferred_element_type=f32)
    sigma = jax.nn.sigmoid(gate_part)
    act = gate_part * sigma
    inner = act * up_part
    d_inner = raw * scale
    d_gate = (d_inner * up_part * sigma * (1.0 + gate_part * (1.0 - sigma))).astype(bf16)
    d_up = (d_inner * act).astype(bf16)
    scaled = (inner * scale).astype(bf16)
    out_rows = jnp.einsum("lmf,lfd->lmd", scaled, w_down, preferred_element_type=f32).astype(bf16)
    d_rows = jnp.einsum("lmf,ldf->lmd", d_gate, w_gate, preferred_element_type=f32)
    d_rows = (d_rows + jnp.einsum("lmf,ldf->lmd", d_up, w_up, preferred_element_type=f32)).astype(bf16)
    slot_d_gate = branch_scale * jnp.sum(inner * raw, axis=2)
    shape4 = (local, shards, CAP, width)
    mix = jnp.einsum("blst,lbsd->btd", one_hot, out_rows.reshape(shape4), preferred_element_type=f32)
    d_in = jnp.einsum("blst,lbsd->btd", one_hot, d_rows.reshape(shape4), preferred_element_type=f32)
    dg = jnp.sum(jnp.where(here, slot_d_gate.reshape(local, shards, CAP).transpose(1, 0, 2)[..., None], 0.0), axis=2)
    dg_all = jnp.zeros((shards, count, LANES), f32)
    dg_all = lax.dynamic_update_slice(dg_all, dg.transpose(0, 2, 1), (0, 0, first))
    back = jnp.concatenate([mix, d_in, dg_all], axis=2).astype(bf16).reshape(shards * count, -1)
    back = lax.psum_scatter(back, "shard", scatter_dimension=0, tiled=True).astype(f32)
    return back[:, :width], back[:, width:2 * width], back[:, 2 * width:2 * width + gates.shape[1]].T


def body(
    tokens, prefix, routes, cotangent, w_query, key_weight, value_weight, w_out,
    norm_attn, norm_moe, w_router, w_gate, w_up, w_down,
):
    count, width = tokens.shape
    local, _, hidden = w_gate.shape
    shards, reps = lax.axis_size("shard"), lax.axis_size("rep")
    experts = local * shards
    kv_width = key_weight.shape[1]
    me, rep = lax.axis_index("shard"), lax.axis_index("rep")
    group = QUERY_HEADS // KEY_VALUE_HEADS
    spread = reps <= MOST_GATHERED
    axes = ("rep", "shard") if spread else "shard"
    all_cot = lax.all_gather(cotangent, axes, axis=0).reshape(-1, count, width)
    cosine, sine = rotary_tables(count)
    mine = pack(w_query, key_weight, value_weight, w_out, w_router, norm_attn, norm_moe)
    packed, query, keys, values, attended, hidden_one, normed_two, gates, normed_one = front(
        tokens, prefix, routes.T, mine, cosine, sine, experts, kv_width
    )
    packed = packed.reshape(width, -1)
    cuts = [width, width + kv_width, width + 2 * kv_width, 2 * width + 2 * kv_width]
    wo, small = packed[:, cuts[2]:cuts[3]], packed[:, cuts[3]:]
    wr = small[:, :experts]
    gain_one = small[:, experts].astype(f32)[None, :]
    gain_two = small[:, experts + 1].astype(f32)[None, :]
    all_x = lax.all_gather(normed_two, axes, axis=0).reshape(-1, count, width)
    all_gates = lax.all_gather(gates, axes, axis=0).reshape(-1, experts, count)
    own = rep * shards if spread else 0
    rows = lambda a: lax.dynamic_slice_in_dim(a, own, shards, axis=0)
    mix, d_in, d_gates = own_part(rows(all_x), rows(all_cot), rows(all_gates), me * local, w_gate, w_up, w_down)
    sums = moe_sums(all_x, all_cot, all_gates, w_gate, w_up, w_down)
    if not spread:
        sums = [lax.psum(a.astype(bf16), "rep").astype(f32) for a in sums]
    d_w_gate, d_w_up, d_w_down = sums

    inputs = tokens.astype(f32)
    cot = cotangent.astype(f32)
    scale_one, scale_two = norm_scale(inputs), norm_scale(hidden_one)
    result = (hidden_one + mix).astype(bf16)
    d_logits = (gates * (d_gates - jnp.sum(gates * d_gates, axis=0, keepdims=True))).astype(bf16)
    d_router = dot(normed_two, d_logits, ((0,), (1,)))
    d_normed_two = d_in + dot(d_logits, wr, ((0,), (1,)))
    d_hidden, d_gain_two = norm_backward(hidden_one, scale_two, gain_two, d_normed_two)
    d_hidden = d_hidden + cot
    d_projected = (branch_scale * d_hidden).astype(bf16)
    d_wo = dot(attended, d_projected, ((0,), (0,)))
    d_attended = dot(d_projected, wo, ((1,), (1,))).astype(bf16)
    query4 = query.reshape(count, KEY_VALUE_HEADS, group, HEAD_SIZE)
    keys3 = keys.reshape(count, KEY_VALUE_HEADS, HEAD_SIZE)
    values3 = values.reshape(count, KEY_VALUE_HEADS, HEAD_SIZE)
    raw = jnp.einsum("tngd,snd->ngts", query4, keys3, preferred_element_type=f32)
    place = jnp.arange(count, dtype=jnp.int32)
    visible = (place[None, :] <= place[:, None]) | (place[None, :] < prefix[0])
    probs = jax.nn.softmax(jnp.where(visible, raw * score_scale, masked_value), axis=-1)
    d_attended = d_attended.reshape(count, KEY_VALUE_HEADS, group, HEAD_SIZE)
    d_values = jnp.einsum("ngts,tngd->snd", probs.astype(bf16), d_attended, preferred_element_type=f32)
    d_probs = jnp.einsum("tngd,snd->ngts", d_attended, values3, preferred_element_type=f32)
    weighted = jnp.sum(probs * d_probs, axis=-1, keepdims=True)
    d_scores = (probs * (d_probs - weighted) * score_scale).astype(bf16)
    d_query = jnp.einsum("ngts,snd->tngd", d_scores, keys3, preferred_element_type=f32)
    d_keys = jnp.einsum("ngts,tngd->snd", d_scores, query4, preferred_element_type=f32)
    d_query = turn_back(d_query.reshape(count, -1), cosine, sine).astype(bf16)
    d_keys = turn_back(d_keys.reshape(count, -1), cosine, sine).astype(bf16)
    d_values = d_values.reshape(count, -1).astype(bf16)
    d_qkv = jnp.concatenate([d_query, d_keys, d_values], axis=1)
    d_w_qkv = dot(normed_one, d_qkv, ((0,), (0,)))
    d_normed_one = dot(d_qkv, packed[:, :cuts[2]], ((1,), (1,)))
    d_tokens, d_gain_one = norm_backward(inputs, scale_one, gain_one, d_normed_one)
    d_tokens = d_tokens + d_hidden
    small = jnp.concatenate([d_router, d_gain_one.T, d_gain_two.T], axis=1)
    small = jnp.pad(small, ((0, 0), (0, LANES - small.shape[1])))
    shares = jnp.concatenate([d_w_qkv, d_wo, small], axis=1).astype(bf16)
    shares = lax.psum_scatter(shares, "shard", scatter_dimension=0, tiled=True)
    totals = lax.psum(shares, "rep").astype(f32)
    d_wq, d_wk, d_wv, d_wo, small = jnp.split(totals, cuts, axis=1)
    return (
        result, d_tokens, d_wq, d_wk, d_wv, d_wo, small[:, experts], small[:, experts + 1],
        small[:, :experts], d_w_gate, d_w_up, d_w_down,
    )


def solution(mesh):
    rows = P(("rep", "shard"), None)
    one, two, three = P("shard"), P("shard", None), P("shard", None, None)
    return jax.shard_map(
        body,
        mesh=mesh,
        in_specs=(rows, P(("rep", "shard")), rows, rows, two, two, two, two, one, one, two, three, three, three),
        out_specs=(rows, rows, two, two, two, two, one, one, two, three, three, three),
        check_vma=False,
    )
```

time: 844 us -> 803 us (0.951)
  matrix products: 415 us -> 132 us
  Pallas kernels: 0 us -> 201 us
  waiting for transfers between devices: 285 us -> 385 us
  local copies, waits for them, and re-layouts: 73.7 us -> 37 us
  other arithmetic: 45.3 us -> 23.6 us
    dot_general x43 -> x12, matrix products: 367 us -> 92.9 us  [the longest x1 14.1 us: own_part(): jnp.einsum('lmf,ldf->lmd', d_gate, w_gate, preferred_element_type=f32)]
    pallas_call x0 -> x2, Pallas kernels: none -> 201 us  [the longest x1 144 us: moe_sums(): pl.pallas_call(functools.partial(sums_kernel, nb), out_shape=[jax.ShapeDt...]
    reduce_scatter x1, waiting for transfers between devices: 0.01 us -> 63.1 us  [body(): shares = lax.psum_scatter(shares, 'shard', scatter_dimension=0, tiled=True)]
    reduce_scatter x1, waiting for transfers between devices: 0.01 us -> 57.7 us  [own_part(): lax.psum_scatter(back, 'shard', scatter_dimension=0, tiled=True).astype(f32)]
    transpose x18 -> x3, local copies, waits for them, and re-layouts: 34.7 us -> 1.93 us  [the longest x1 1.14 us: own_part(): xg = jnp.einsum('blst,btd->lbsd', one_hot, x).reshape(local, -1, width)]
    psum x1, waiting for transfers between devices: 27.6 us -> 0.01 us  [body(): totals = lax.psum(shares, 'rep').astype(f32)]
    squeeze x1 -> x0, local copies, waits for them, and re-layouts: 13 us -> none  [gathered(): lax.dynamic_index_in_dim(arrived, number, 0, keepdims=False)[..., :width]]
    concatenate x2 -> x4, local copies, waits for them, and re-layouts: 1.01 us -> 13 us  [the longest x2 12.9 us: own_part(): jnp.concatenate([mix, d_in, dg_all], axis=2).astype(bf16)]
  transfers between devices with their start and end apart: 6 -> 6, of which waited for: 4 -> 5; matrix products, arithmetic and copies ran while one was open for 31% -> 5% of each run, Pallas kernels for 0% -> 18%
where the time goes in v2:
time: 803 us; the launch traced here: 795 us
  waiting for transfers between devices  385 us (48%)
  Pallas kernels  201 us (25%)
  matrix products  132 us (16%)
  local copies, waits for them, and re-layouts  37 us (5%)
  other arithmetic  23.6 us (3%)
  between operations  15.4 us (2%)
    pallas_call x1, Pallas kernels, moe_sums(): pl.pallas_call(functools.partial(sums_kernel, nb), out_shape=[jax.ShapeDt...  144 us
    all_gather x1, waiting for transfers between devices, body(): all_x = lax.all_gather(normed_two, axes, axis=0).reshape(-1, count, width)  116 us
    all_gather x1, waiting for transfers between devices, body(): all_cot = lax.all_gather(cotangent, axes, axis=0).reshape(-1, count, width)  96.1 us
    reduce_scatter x1, waiting for transfers between devices, body(): shares = lax.psum_scatter(shares, 'shard', scatter_dimension=0, tiled=True)  63.1 us
    reduce_scatter x1, waiting for transfers between devices, own_part(): lax.psum_scatter(back, 'shard', scatter_dimension=0, tiled=True).astype(f32)  57.7 us
    pallas_call x1, Pallas kernels, front(): pl.pallas_call(front_kernel, out_shape=[sds((shards, depth, total), bf16)...  56.8 us
    all_gather x1, waiting for transfers between devices, body(): all_gates = lax.all_gather(gates, axes, axis=0).reshape(-1, experts, count)  51.4 us
  transfers between devices with their start and end apart: 6, of which 5 were waited for; matrix products, arithmetic and copies ran while one was open for 5% of the time, Pallas kernels for 18%

profile of v2, /device:TPU:0, one launch (start us, length us, event | category | flops | bytes accessed | tf_op | source)
XLA Modules:
  0.0 794.6 jit_solution(7774713087785774887)
XLA Ops:
  9.6 1.0 constant_dynamic-update-slice_fusion.3
  13.3 1.0 constant_dynamic-update-slice_fusion
  15.2 56.8 %front.1 = (bf16[8,128,3200]{2,1,0:T(8,128)(2,1)}, bf16[256,1024]{1,0:T(8,128)(2,1)}, bf16[256,512]{1,0:T(8,128)(2,1)}, bf16[256,512]{1,0:T(8,128)(2,1)}, bf16[2...) custom-call(s32[1]{0:T(128)} %copy.238.prefix_ref, ...), custom_call_target="tpu_custom_call" | custom-call | tf_op jit(solution)/shard_map/front/pallas_call | solution.py:314
  73.6 51.4 %all-gather.7.cloned.1.call-done = f32[1024,256]{1,0:T(8,128)} async-done(((f32[32,256]{1,0:T(8,128)}), f32[1024,256]{1,0:T(8,128)}) %all-gather.7.cloned.1.call-update) | async-done | bytes 1048592 | tf_op jit(solution)/shard_map/all_gather | solution.py:425
  125.0 0.9 broadcast_compare_fusion
  126.1 115.6 %all-gather.9.cloned.1.call-done = bf16[8192,1024]{1,0:T(8,128)(2,1)} async-done(((bf16[256,1024]{1,0:T(8,128)(2,1)}), bf16[8192,1024]{1,0:T(8,128)(2,1)}) %all-gather.9.cloned.1.call-update) | async-done | bytes 16777232 | tf_op jit(solution)/shard_map/all_gather | solution.py:424
  241.7 4.0 fusion.30
  245.7 1.1 copy.158
  246.9 8.8 %fusion.111 = f32[4,768,512]{1,2,0:T(8,128)} fusion(bf16[4,768,1024]{2,1,0:T(8,128)(2,1)S(1)} %bitcast.154, bf16[4,1024,512]{2,1,0:T(8,128)(2,1)} %wg_hbm.1), kind=kOutput, calls=%fused_computation.151 | convolution fusion | flops 3221225472 | bytes 16777216 | tf_op jit(solution)/shard_map/lmd,ldf->lmf/dot_general | solution.py:374
  255.7 5.9 fusion.112
  261.6 96.1 %all-gather.11.cloned.1.call-done = bf16[8192,1024]{1,0:T(8,128)(2,1)} async-done(((bf16[256,1024]{1,0:T(8,128)(2,1)}), bf16[8192,1024]{1,0:T(8,128)(2,1)}) %all-gather.11.cloned.1.call-update) | async-done | bytes 16777232 | tf_op jit(solution)/shard_map/all_gather | solution.py:412
  357.7 4.0 fusion.35
  362.5 12.7 %multiply_reduce_fusion = (f32[4,768]{1,0:T(4,128)S(1)}, f32[4,768,512]{1,2,0:T(8,128)}) fusion(f32[4,768,512]{1,2,0:T(8,128)} %fusion.112, f32[4,768,512]{1,2,0:T(8,128)} %fusion.111, bf16[4,768,1024]{2,1,0:T(8,128)(2,1)S(1)} %bitcast.153, bf16[4,512,1024]{2,1,0:T(8,128)(2,1)} %wd_hbm.1), kind=kOutput, calls=%fused_computation.13 | convolution fusion | flops 3232232448 | bytes 29372416 | tf_op jit(solution)/shard_map/lmd,lfd->lmf/dot_general | solution.py:376
  375.3 2.3 select_reduce_fusion.1
  377.6 12.1 %convolution_convert_fusion.1 = bf16[4,768,1024]{2,1,0:T(8,128)(2,1)} fusion(bf16[4,512,1024]{2,1,0:T(8,128)(2,1)} %wd_hbm.1, f32[4,768]{1,0:T(4,128)S(1)} %mul.399, f32[4,768,512]{1,2,0:T(8,128)} %fusion.112, f32[4,768,512]{1,2,0:T(8,128)} %fusion.111), kind=kOutput, calls=%fused_computation.35 | convolution fusion | flops 3235381248 | bytes 23080960 | tf_op jit(solution)/shard_map/lmf,lfd->lmd/dot_general | solution.py:384
  389.7 7.2 bitcast_convert_fusion.1
  396.9 6.4 copy.216
  403.3 14.1 %fusion.23 = f32[4,768,1024]{2,1,0:T(8,128)} fusion(bf16[4,1024,512]{2,1,0:T(8,128)(2,1)} %wg_hbm.1, f32[4,768,512]{1,2,0:T(8,128)} %fusion.111, f32[4,768,512]{1,2,0:T(8,128)} %fusion.112, f32[4,768,512]{1,2,0:T(8,128)} %get-tuple-element.113, f32[4,768]{1,0:T(4,128)S(1)} %mul.399), kind=kOutput, calls=%fused_computation.42 | convolution fusion | flops 3238526976 | bytes 35663872 | tf_op jit(solution)/shard_map/lmf,ldf->lmd/dot_general | solution.py:385
  417.4 13.8 %add_convert_fusion = bf16[4,768,1024]{2,1,0:T(8,128)(2,1)} fusion(f32[4,768,1024]{2,1,0:T(8,128)} %fusion.23, bf16[4,1024,512]{2,1,0:T(8,128)(2,1)} %wu_hbm.1, f32[4,768,512]{1,2,0:T(8,128)} %get-tuple-element.113, f32[4,768]{1,0:T(4,128)S(1)} %mul.399, f32[4,768,512]{1,2,0:T(8,128)} %fusion.111), kind=kOutput, calls=%fused_computation.4 | convolution fusion | flops 3238526976 | bytes 35663872 | tf_op jit(solution)/shard_map/lmf,ldf->lmd/dot_general | solution.py:386
  431.2 7.2 bitcast_convert_fusion
  438.4 6.4 copy.217
  445.0 7.3 pad_maximum_fusion
  453.3 1.0 copy.181
  454.5 1.3 slice_convert_fusion
  456.4 1.1 copy.176
  457.4 2.1 copy.175
  459.5 1.8 copy.174
  462.0 4.7 fusion.110
  466.7 57.7 %reduce-scatter.3.cloned.1.call-done = bf16[256,2176]{0,1:T(8,128)(2,1)} async-done(((bf16[2048,2176]{0,1:T(8,128)(2,1)}), bf16[256,2176]{0,1:T(8,128)(2,1)}) %reduce-scatter.3.cloned.1.call-update) | async-done | bytes 1114128 | tf_op jit(solution)/shard_map/reduce_scatter | solution.py:395
  524.4 1.5 convert_element_type.97
  526.0 1.7 multiply_reduce_fusion.1
  528.1 2.3 fusion.66
  530.6 2.8 fusion.113
  533.4 8.3 %fusion.57 = f32[8,64,2,256]{3,1,2,0:T(8,128)} fusion(bf16[256,8,64,1]{0,2,3,1:T(8,128)(2,1)} %bitcast.177, f32[8,256,256,2]{2,1,3,0:T(8,128)} %fusion.113, f32[8,2,256,256]{2,3,1,0:T(8,128)} %get-tuple-element.116, f32[8,2,256]{2,1,0:T(2,128)S(1)} %get-tuple-element.115), kind=kOutput, calls=%fused_computation.58 | convolution fusion | flops 141562112 | bytes 9715712 | tf_op jit(solution)/shard_map/ngts,snd->tngd/dot_general | solution.py:458
  541.7 7.9 fusion.69
  549.6 3.1 fusion.73
  552.7 1.0 convolution_convert_fusion.3
  554.1 3.3 convolution_convert_fusion
  557.4 4.5 fusion.82
  562.1 2.0 convolution_convert_fusion.2
  564.2 5.5 fusion.3
  569.7 63.1 %reduce-scatter.5.cloned.1.call-done = bf16[128,3200]{1,0:T(8,128)(2,1)} async-done(((bf16[1024,3200]{1,0:T(8,128)(2,1)}), bf16[128,3200]{1,0:T(8,128)(2,1)}) %reduce-scatter.5.cloned.1.call-update) | async-done | bytes 819216 | tf_op jit(solution)/shard_map/reduce_scatter | solution.py:471
  632.8 144.4 %expert_sums.1 = (f32[4,1024,512]{2,1,0:T(8,128)}, f32[4,1024,512]{2,1,0:T(8,128)}, f32[4,512,1024]{2,1,0:T(8,128)}) custom-call(bf16[32,256,1024]{2,1,0:T(8,128)(2,1)} %bitcast.150, bf16[32,256,1024]{2,1,0:T(8,128)(2,1)} %bitcast.152, f32[32,32,256]{2,1,0:T(8,128)} %bitcast.165, bf16[4,1024,512]{2,1,0:T(8,128)(2,1)} %wg_hbm.1, ...), custom_call_target="tpu_custom_call" | custom-call | tf_op jit(solution)/shard_map/expert_sums/pallas_call | solution.py:128
  777.3 1.5 fusion.79
  778.8 1.3 copy.193
  780.1 1.0 copy.192
  781.1 1.3 convert_element_type.115
  784.6 2.1 fusion.108
  (92 shorter events, 14.8 us)
Async XLA Ops:
  7.2 117.9 %all-gather.7.cloned.1.call-start = ((), (), s32[]{:S(2)}) async-start(), calls=%async_computation.5 | async-start | bytes 1081344 | tf_op jit(solution)/shard_map/all_gather | solution.py:425
  14.3 0.9 copy-start.8
  72.1 169.7 %all-gather.9.cloned.1.call-start = ((), (), s32[]{:S(2)}) async-start(), calls=%async_computation.6 | async-start | bytes 17301504 | tf_op jit(solution)/shard_map/all_gather | solution.py:424
  72.8 284.9 %all-gather.11.cloned.1.call-start = ((), (), s32[]{:S(2)}) async-start(), calls=%async_computation.7 | async-start | bytes 17301504 | tf_op jit(solution)/shard_map/all_gather | solution.py:412
  73.5 450.9 %reduce-scatter.3.cloned.1.call-start = ((), (), s32[]{:S(2)}) async-start(), calls=%async_computation.2 | async-start | bytes 10027008 | tf_op jit(solution)/shard_map/reduce_scatter | solution.py:395
  246.9 8.8 %copy-start.2 = (bf16[4,1024,512]{2,1,0:T(8,128)(2,1)S(1)}, bf16[4,1024,512]{2,1,0:T(8,128)(2,1)}, u32[]{:S(2)}) copy-start(bf16[4,1024,512]{2,1,0:T(8,128)(2,1)} %wu_hbm.1) | copy-start | bytes 12582916
  452.3 1.0 copy-start.6
  452.3 2.0 copy-start.7
  452.3 3.7 copy-start.3
  452.3 180.5 %reduce-scatter.5.cloned.1.call-start = ((), (), s32[]{:S(2)}) async-start(), calls=%async_computation.3 | async-start | bytes 7372800 | tf_op jit(solution)/shard_map/reduce_scatter | solution.py:471
  462.0 63.9 %copy-start.11 = (f32[32,256]{1,0:T(8,128)S(1)}, f32[32,256]{1,0:T(8,128)}, u32[]{:S(2)}) copy-start(f32[32,256]{1,0:T(8,128)} %get-tuple-element.25) | copy-start | bytes 98308
  524.4 3.3 copy-start.4
  525.9 2.2 copy-start.1
  533.4 8.3 %copy-start.12 = (bf16[256,1024]{0,1:T(8,128)(2,1)S(1)}, bf16[256,1024]{0,1:T(8,128)(2,1)}, u32[]{:S(2)}) copy-start(bf16[256,1024]{0,1:T(8,128)(2,1)} %copy.175) | copy-start | bytes 1572868
  549.6 3.1 copy-start.5
  549.6 4.1 copy-start.9
  549.6 4.3 copy-start.13
  552.7 1.4 copy-start.10
  569.7 211.4 %all-reduce.4.cloned.1.call-start = ((), (), s32[]{:S(2)}) async-start(), calls=%async_computation.4 | async-start | bytes 1638400 | tf_op jit(solution)/shard_map/psum | solution.py:472
  781.1 5.6 copy-start
Sparse Core Ops, SparseCore 0:
  72.2 52.8 all-gather.6
  127.9 113.8 all-gather.8
  244.6 113.0 all-gather.10
  452.4 71.9 reduce-scatter.2
  569.8 62.9 reduce-scatter.4
  635.1 44.6 all-reduce.3

commit v3 on v2

--- a/solution.py
+++ b/solution.py
@@ -152,8 +152,8 @@
     return (1 - core) * flip(index, bits[step]) + core * flip(index, bits[-1 - step])
 
 class PlaneGather:
-    def __init__(self, buf, send, recv, base=0):
-        self.buf, self.send, self.recv, self.base = buf, send, recv, base
+    def __init__(self, buf, own, send, recv, base=0):
+        self.buf, self.own, self.send, self.recv, self.base = buf, own, send, recv, base
         self.rep, self.me = lax.axis_index("rep"), lax.axis_index("shard")
         self.core = self.me % 2
         shards = lax.axis_size("shard")
@@ -170,18 +170,19 @@
                 of = turned(of, self.core, step, self.bits)
         return of
 
-    def copy(self, number, owner, target):
+    def copy(self, number, subset, target):
+        owner = self.owner(self.me, subset)
         return pltpu.make_async_remote_copy(
-            src_ref=self.buf.at[owner], dst_ref=self.buf.at[owner],
+            src_ref=self.buf.at[owner] if subset else self.own, dst_ref=self.buf.at[owner],
             send_sem=self.send.at[self.base + number], recv_sem=self.recv.at[self.base + number],
             device_id=(self.rep, target), device_id_type=MESH,
         )
 
     def chip_copy(self, step, subset):
-        return self.copy((1 << step) - 1 + subset, self.owner(self.me, subset), turned(self.me, self.core, step, self.bits))
+        return self.copy((1 << step) - 1 + subset, subset, turned(self.me, self.core, step, self.bits))
 
     def core_copy(self, subset):
-        return self.copy((1 << self.steps) - 1 + subset, self.owner(self.me, subset), flip(self.me, 1))
+        return self.copy((1 << self.steps) - 1 + subset, subset, flip(self.me, 1))
 
     def start(self):
         for step in range(self.steps):
@@ -199,11 +200,34 @@
     def finish(self):
         for subset in range(1 << self.steps):
             self.core_copy(subset).wait_recv()
+        self.sent()
+
+    def sent(self):
         for step in range(self.steps):
             for subset in range(1 << step):
                 self.chip_copy(step, subset).wait_send()
         for subset in range(1 << self.steps):
             self.core_copy(subset).wait_send()
+
+class RepSends:
+    def __init__(self, buf, own, send, recv, base=0):
+        rep, me, reps = lax.axis_index("rep"), lax.axis_index("shard"), lax.axis_size("rep")
+        self.copies = [
+            pltpu.make_async_remote_copy(
+                src_ref=own, dst_ref=buf.at[rep], send_sem=send.at[base + j - 1], recv_sem=recv.at[base + j - 1],
+                device_id=((rep + j) % reps, me), device_id_type=MESH,
+            )
+            for j in range(1, reps)
+        ]
+
+    def start(self):
+        for copy in self.copies:
+            copy.start()
+
+    def finish(self):
+        for copy in self.copies:
+            copy.wait()
+
 
 def rotate(v, cosine, sine, sign):
     lane = lax.broadcasted_iota(jnp.int32, v.shape, 1) % HEAD_SIZE
@@ -234,9 +258,9 @@
 def lanes(j, count=1):
     return pl.ds(pl.multiple_of(j * LANES * count, LANES), LANES * count)
 
-def front_kernel(prefix_ref, tok_ref, routes_ref, cos_ref, sin_ref, mine_ref,
-                 wall_out, q_out, k_out, v_out, att_out, hid_out, x_out, gates_out, n1_out,
-                 wbuf, qkv_ref, send, recv, lsem):
+def front_kernel(spread, prefix_ref, tok_ref, routes_ref, cos_ref, sin_ref, mine_ref, cot_ref,
+                 wall_out, cown_out, ccol_out, q_out, k_out, v_out, att_out, hid_out, x_out, gates_out, n1_out,
+                 wbuf, qkv_ref, send, recv, csend, crecv, zsend, zrecv, lsem):
     count, width = tok_ref.shape
     kv_width = k_out.shape[1]
     experts = gates_out.shape[0]
@@ -244,14 +268,21 @@
     me = lax.axis_index("shard")
     own = pltpu.make_async_copy(mine_ref, wbuf.at[me], lsem.at[0])
     own.start()
-    gather = PlaneGather(wbuf, send, recv)
+    gather = PlaneGather(wbuf, mine_ref, send, recv)
+    gather.start()
+    far = RepSends(ccol_out, cot_ref, zsend, zrecv)
+    if spread:
+        far.start()
+    near = PlaneGather(cown_out, cot_ref, csend, crecv)
+    own_cot = pltpu.make_async_copy(cot_ref, cown_out.at[me], lsem.at[2])
+    own_cot.start()
     own.wait()
-    gather.start()
     inputs = tok_ref[...].astype(f32)
     scaled = inputs * norm_scale(inputs)
     for step in range(gather.steps):
         gather.forward(step)
     gather.finish()
+    near.start()
     keep = pltpu.make_async_copy(wbuf, wall_out, lsem.at[1])
     keep.start()
     cut = [0, width, width + kv_width, width + 2 * kv_width, 2 * width + 2 * kv_width]
@@ -274,6 +305,8 @@
     v_out[...] = qkv_ref[:, cut[2]:cut[3]].astype(bf16)
     prefix_len = prefix_ref[0]
 
+    near.forward(0)
+
     def head(j, carry):
         keys = one_head_twice(k_out[:, lanes(j // 2)], j % 2)
         values = one_head_twice(v_out[:, lanes(j // 2)], j % 2)
@@ -283,6 +316,8 @@
         att_out[:, lanes(j)] = jnp.where(low, both[:count], both[count:]).astype(bf16)
         return carry
     lax.fori_loop(0, KEY_VALUE_HEADS, head, 0)
+    for step in range(1, near.steps):
+        near.forward(step)
 
     def project_out(j, carry):
         w = wbuf[:, :, pl.ds(pl.multiple_of(cut[3] + j * 2 * LANES, LANES), 2 * LANES)].reshape(shards * depth, 2 * LANES)
@@ -302,30 +337,428 @@
     weights = jnp.where(named, jnp.exp(jnp.where(named, logits - top, 0.0)), 0.0)
     gates_out[...] = weights / jnp.sum(weights, axis=0, keepdims=True)
     keep.wait()
-
-def front(tokens, prefix, routes, mine, cosine, sine, experts, kv_width):
+    near.finish()
+    own_cot.wait()
+    if spread:
+        far.finish()
+
+def front(tokens, prefix, routes, mine, cot, cosine, sine, experts, kv_width, spread):
     count, width = tokens.shape
-    shards = lax.axis_size("shard")
+    shards, reps = lax.axis_size("shard"), lax.axis_size("rep")
     depth, total = mine.shape
     v = pl.BlockSpec(memory_space=pltpu.VMEM)
     any_ = pl.BlockSpec(memory_space=pl.ANY)
     sds = jax.ShapeDtypeStruct
     n = PlaneGather.copies(shards)
     return pl.pallas_call(
-        front_kernel,
+        functools.partial(front_kernel, spread),
         out_shape=[
-            sds((shards, depth, total), bf16), sds((count, width), bf16), sds((count, kv_width), bf16), sds((count, kv_width), bf16),
+            sds((shards, depth, total), bf16), sds((shards, count, width), bf16), sds((reps, count, width), bf16), sds((count, width), bf16), sds((count, kv_width), bf16), sds((count, kv_width), bf16),
             sds((count, width), bf16), sds((count, width), f32), sds((count, width), bf16), sds((experts, count), f32), sds((count, width), bf16),
         ],
-        in_specs=[pl.BlockSpec(memory_space=pltpu.SMEM), v, v, v, v, any_],
-        out_specs=[any_] + [v] * 8,
+        in_specs=[pl.BlockSpec(memory_space=pltpu.SMEM), v, v, v, v, any_, any_],
+        out_specs=[any_] * 3 + [v] * 8,
         scratch_shapes=[
             pltpu.VMEM((shards, depth, total), bf16), pltpu.VMEM((count, width + 2 * kv_width), f32),
-            pltpu.SemaphoreType.DMA((n,)), pltpu.SemaphoreType.DMA((n,)), pltpu.SemaphoreType.DMA((2,)),
+            *[pltpu.SemaphoreType.DMA((k,)) for k in (n, n, n, n, reps, reps, 3)],
         ],
         compiler_params=pltpu.CompilerParams(vmem_limit_bytes=60 << 20, has_side_effects=True),
         name="front",
-    )(prefix, tokens, routes, cosine, sine, mine)
+    )(prefix, tokens, routes, cosine, sine, mine, cot)
+
+def share_order(steps):
+    groups = [[u for u in range(1 << steps) if u % (2 << k) == 1 << k] for k in range(steps)]
+    return groups + [[0]]
+
+
+class PlaneReduce:
+    def __init__(self, mine, theirs, from_core, from_chip, csend, crecv, send, recv):
+        self.mine, self.theirs, self.from_core, self.from_chip = mine, theirs, from_core, from_chip
+        self.csend, self.crecv, self.send, self.recv = csend, crecv, send, recv
+        self.rep, self.me = lax.axis_index("rep"), lax.axis_index("shard")
+        self.core = self.me % 2
+        self.bits = [1 << i for i in range(1, lax.axis_size("shard").bit_length() - 1)]
+        self.steps = len(self.bits)
+
+    def owner(self, core, u):
+        at = flip(self.me, 1) if core else self.me
+        of = (1 - self.core) if core else self.core
+        for step in range(self.steps):
+            if u >> step & 1:
+                at = turned(at, of, step, self.bits)
+        return at
+
+    def core_copy(self, u):
+        return pltpu.make_async_remote_copy(
+            src_ref=self.theirs.at[u], dst_ref=self.from_core.at[u], send_sem=self.csend.at[u], recv_sem=self.crecv.at[u],
+            device_id=(self.rep, flip(self.me, 1)), device_id_type=MESH,
+        )
+
+    def slot(self, step, u):
+        return (1 << self.steps) - (1 << (self.steps - step)) + (u >> (step + 1))
+
+    def chip_copy(self, step, u):
+        slot = self.slot(step, u)
+        return pltpu.make_async_remote_copy(
+            src_ref=self.mine.at[u], dst_ref=self.from_chip.at[slot], send_sem=self.send.at[slot], recv_sem=self.recv.at[slot],
+            device_id=(self.rep, turned(self.me, self.core, step, self.bits)), device_id_type=MESH,
+        )
+
+    def total(self, u, before, rows):
+        whole = self.mine[u, rows].astype(f32) + self.from_core[u, rows].astype(f32)
+        for step in range(before):
+            whole = whole + self.from_chip[self.slot(step, u), rows].astype(f32)
+        return whole
+
+    def send_on(self, step, u):
+        self.core_copy(u).wait_recv()
+        count = self.mine.shape[1]
+        piece = 32
+
+        def add(i, carry):
+            rows = pl.ds(pl.multiple_of(i * piece, piece), piece)
+            self.mine[u, rows] = self.total(u, step, rows).astype(bf16)
+            return carry
+        lax.fori_loop(0, count // piece, add, 0)
+        self.chip_copy(step, u).start()
+
+    def arrive(self, step):
+        for u in range(1 << self.steps):
+            if u % (2 << step) == 1 << step:
+                self.chip_copy(step, u).wait_recv()
+
+    def last(self, out):
+        self.core_copy(0).wait_recv()
+        count = self.mine.shape[1]
+        piece = 32
+
+        def add(i, carry):
+            rows = pl.ds(pl.multiple_of(i * piece, piece), piece)
+            out[rows] = self.total(0, self.steps, rows)
+            return carry
+        lax.fori_loop(0, count // piece, add, 0)
+
+    def finish(self):
+        for u in range(1 << self.steps):
+            self.core_copy(u).wait_send()
+        for step in range(self.steps):
+            for u in range(1 << self.steps):
+                if u % (2 << step) == 1 << step:
+                    self.chip_copy(step, u).wait_send()
+
+
+def own_kernel(spread, nb, x_ref, gates_ref, c_hbm, wg_hbm, wu_hbm, wd_hbm,
+               xown_out, xcol_out, gown_out, gcol_out, back_out, dg_out,
+               wg, wu, wd, xb, cb, xg_ref, cg_ref, sg_ref, y_ref, ds_ref, mine, theirs, from_core, from_chip,
+               gown, gcol, dgs, dgr,
+               xs, xr, zxs, zxr, zgs, zgr, gs, gr, dss, dsr, css, csr, hs, hr, wsem, bsem, lsem):
+    count, width = x_ref.shape
+    local, _, hidden = wg.shape
+    rep, me = lax.axis_index("rep"), lax.axis_index("shard")
+    shards = lax.axis_size("shard")
+    first = me * local
+    near = PlaneGather(xown_out, x_ref, xs, xr)
+    near.start()
+    gown[me] = gates_ref[...]
+
+    def peer(j):
+        return (rep, (me + j) % shards)
+
+    gate_sends = [
+        pltpu.make_async_remote_copy(
+            src_ref=gates_ref, dst_ref=gown.at[me], send_sem=gs.at[j - 1], recv_sem=gr.at[j - 1],
+            device_id=peer(j), device_id_type=MESH,
+        )
+        for j in range(1, shards)
+    ]
+    for copy in gate_sends:
+        copy.start()
+    far = [RepSends(xcol_out, x_ref, zxs, zxr), RepSends(gcol, gates_ref, zgs, zgr)] if spread else []
+    for sends in far:
+        sends.start()
+    own_x = pltpu.make_async_copy(x_ref, xown_out.at[me], lsem)
+    own_x.start()
+    weights = [pltpu.make_async_copy(a, b, wsem.at[i]) for i, (a, b) in enumerate(((wg_hbm, wg), (wu_hbm, wu), (wd_hbm, wd)))]
+    for copy in weights:
+        copy.start()
+    reduce = PlaneReduce(mine, theirs, from_core, from_chip, css, csr, hs, hr)
+    for copy in gate_sends:
+        copy.wait_recv()
+    for step in range(near.steps):
+        near.forward(step)
+    own_x.wait()
+    for subset in range(1 << near.steps):
+        near.core_copy(subset).wait_recv()
+    for copy in weights:
+        copy.wait()
+
+    groups = share_order(reduce.steps)
+    order = [u for group in groups for u in group]
+    half = nb // 2
+    dg_sends = []
+
+    def fetch(at, slot):
+        return (pltpu.make_async_copy(xown_out.at[at], xb.at[slot], bsem.at[0, slot]),
+                pltpu.make_async_copy(c_hbm.at[at], cb.at[slot], bsem.at[1, slot]))
+
+    plan = []
+    for q in range(len(order) // half):
+        for u in order[q * half:(q + 1) * half]:
+            plan += [(1, u), (0, u)]
+    owners = [reduce.owner(core, u) for core, u in plan]
+    for copy in fetch(owners[0], 0):
+        copy.start()
+    for q in range(len(order) // half):
+        for b in range(nb):
+            n = q * nb + b
+            if n + 1 < len(plan):
+                for copy in fetch(owners[n + 1], (n + 1) % 2):
+                    copy.start()
+            for copy in fetch(owners[n], n % 2):
+                copy.wait()
+            gather_block(xb[n % 2], cb[n % 2], gown[owners[n]], first, local, xg_ref, cg_ref, sg_ref, b * CAP)
+
+        def expert(l, carry):
+            inner, raw, d_gate, d_up, scaled = expert_parts(xg_ref[l], cg_ref[l], sg_ref[l], wg[l], wu[l], wd[l])
+            ds_ref[l] = branch_scale * jnp.sum(inner * raw, axis=1, keepdims=True)
+            rows = pl.ds(pl.multiple_of(l * CAP, CAP), CAP)
+            out = dot(scaled, wd[l]).astype(bf16)
+            d_in = (dot(d_gate, wg[l], ((1,), (1,))) + dot(d_up, wu[l], ((1,), (1,)))).astype(bf16)
+            for b in range(nb):
+                y_ref[b, rows, :width] = out[b * CAP:(b + 1) * CAP]
+                y_ref[b, rows, width:] = d_in[b * CAP:(b + 1) * CAP]
+            return carry
+        lax.fori_loop(0, local, expert, 0)
+        for b in range(nb):
+            core, u = plan[q * nb + b]
+            at = owners[q * nb + b]
+            parts = slot_one_hot(slot_ranks(gown[at]), first, local)
+            table = jnp.concatenate(parts, axis=0).astype(bf16)
+            (theirs if core else mine)[u] = dot(table, y_ref[b], ((0,), (0,))).astype(bf16)
+            if core:
+                reduce.core_copy(u).start()
+            dgs[at] = jnp.concatenate(
+                [jnp.sum(parts[l] * ds_ref[l, b * CAP:(b + 1) * CAP], axis=0, keepdims=True) for l in range(local)], axis=0
+            )
+        for step, group in enumerate(groups[:-1]):
+            done = order[:(q + 1) * half]
+            fresh = order[q * half:(q + 1) * half]
+            if group[-1] in fresh:
+                if step:
+                    reduce.arrive(step - 1)
+                for u in group:
+                    reduce.send_on(step, u)
+    for j in range(1, shards):
+        copy = pltpu.make_async_remote_copy(
+            src_ref=dgs.at[(me + j) % shards], dst_ref=dgr.at[me], send_sem=dss.at[j - 1], recv_sem=dsr.at[j - 1],
+            device_id=peer(j), device_id_type=MESH,
+        )
+        copy.start()
+        dg_sends.append(copy)
+    dgr[me] = dgs[me]
+    gown_out[...] = gown[...]
+    reduce.arrive(reduce.steps - 1)
+    reduce.last(back_out)
+    for copy in dg_sends:
+        copy.wait()
+    dg_out[...] = dgr[...]
+    reduce.finish()
+    near.sent()
+    for copy in gate_sends:
+        copy.wait_send()
+    for sends in far:
+        sends.finish()
+    if spread:
+        gcol_out[...] = gcol[...]
+
+
+def moe_own(x, gates, c, wg, wu, wd, spread, nb=4):
+    count, width = x.shape
+    local, _, hidden = wg.shape
+    shards, reps = lax.axis_size("shard"), lax.axis_size("rep")
+    experts = local * shards
+    v = pl.BlockSpec(memory_space=pltpu.VMEM)
+    any_ = pl.BlockSpec(memory_space=pl.ANY)
+    sds = jax.ShapeDtypeStruct
+    n = PlaneGather.copies(shards)
+    rows = nb * CAP
+    half = shards // 2
+    dma = lambda *k: pltpu.SemaphoreType.DMA(k)
+    return pl.pallas_call(
+        functools.partial(own_kernel, spread, nb),
+        out_shape=[
+            sds((shards, count, width), bf16), sds((reps, count, width), bf16), sds((shards, experts, count), f32),
+            sds((reps, experts, count), f32), sds((count, 2 * width), f32), sds((shards, local, count), f32),
+        ],
+        in_specs=[v, v, any_, any_, any_, any_],
+        out_specs=[any_, any_, v, v, v, v],
+        scratch_shapes=[
+            pltpu.VMEM(wg.shape, bf16), pltpu.VMEM(wu.shape, bf16), pltpu.VMEM(wd.shape, bf16),
+            pltpu.VMEM((2, count, width), bf16), pltpu.VMEM((2, count, width), bf16),
+            pltpu.VMEM((local, rows, width), bf16), pltpu.VMEM((local, rows, width), bf16), pltpu.VMEM((local, rows, 1), f32),
+            pltpu.VMEM((nb, local * CAP, 2 * width), bf16), pltpu.VMEM((local, rows, 1), f32),
+            pltpu.VMEM((half, count, 2 * width), bf16), pltpu.VMEM((half, count, 2 * width), bf16),
+            pltpu.VMEM((half, count, 2 * width), bf16), pltpu.VMEM((half - 1, count, 2 * width), bf16),
+            pltpu.VMEM((shards, experts, count), f32), pltpu.VMEM((reps, experts, count), f32),
+            pltpu.VMEM((shards, local, count), f32), pltpu.VMEM((shards, local, count), f32),
+            dma(n), dma(n), dma(reps), dma(reps), dma(reps), dma(reps), dma(shards), dma(shards), dma(shards), dma(shards),
+            dma(half), dma(half), dma(half), dma(half), dma(3), dma(2, 2), pltpu.SemaphoreType.DMA,
+        ],
+        compiler_params=pltpu.CompilerParams(vmem_limit_bytes=60 << 20, has_side_effects=True),
+        name="own_experts",
+    )(x, gates, c, wg, wu, wd)
+
+def spread_kernel(nb, xown_hbm, cown_hbm, xcol_hbm, ccol_hbm, gown_ref, gcol_ref, wg_hbm, wu_hbm, wd_hbm,
+                  xoth_hbm, coth_hbm, og_hbm, ou_hbm, od_hbm,
+                  xbuf, cbuf, wg, wu, wd, ag, au, ad, xg_ref, cg_ref, sg_ref, goth, send, recv, bsem, wsem, lsem):
+    local = wg.shape[0]
+    shards = gown_ref.shape[0]
+    rep, me = lax.axis_index("rep"), lax.axis_index("shard")
+    reps = lax.axis_size("rep")
+    first = me * local
+    chunks = shards // nb
+
+    def gathers(j):
+        other = (rep + j) % reps
+        return [
+            PlaneGather(buf.at[j - 1], own.at[other], send.at[j - 1, i], recv.at[j - 1, i])
+            for i, (buf, own) in enumerate(((xoth_hbm, xcol_hbm), (coth_hbm, ccol_hbm), (goth, gcol_ref)))
+        ]
+
+    def own_copies(j):
+        other = (rep + j) % reps
+        return (pltpu.make_async_copy(xcol_hbm.at[other], xoth_hbm.at[j - 1, me], lsem.at[0]),
+                pltpu.make_async_copy(ccol_hbm.at[other], coth_hbm.at[j - 1, me], lsem.at[1]))
+
+    def begin(j):
+        for gather in gathers(j):
+            gather.start()
+        for copy in own_copies(j):
+            copy.start()
+        goth[j - 1, me] = gcol_ref[(rep + j) % reps]
+        for copy in own_copies(j):
+            copy.wait()
+
+    def forward(j):
+        for gather in gathers(j):
+            gather.forward(0)
+
+    def end(j):
+        for gather in gathers(j):
+            for step in range(1, gather.steps):
+                gather.forward(step)
+        for gather in gathers(j):
+            gather.finish()
+
+    def fetch(x, c, q, slot):
+        return (pltpu.make_async_copy(x.at[pl.ds(q * nb, nb)], xbuf.at[slot], bsem.at[0, slot]),
+                pltpu.make_async_copy(c.at[pl.ds(q * nb, nb)], cbuf.at[slot], bsem.at[1, slot]))
+
+    def replica(x, c, g, between):
+        for copy in fetch(x, c, 0, 0):
+            copy.start()
+
+        def chunk(q, carry):
+            slot = lax.rem(q, 2)
+
+            @pl.when(q + 1 < chunks)
+            def _():
+                for copy in fetch(x, c, q + 1, 1 - slot):
+                    copy.start()
+            for copy in fetch(x, c, q, slot):
+                copy.wait()
+
+            def block(b, carry):
+                gather_block(xbuf[slot, b], cbuf[slot, b], g[q * nb + b], first, local, xg_ref, cg_ref, sg_ref,
+                             pl.multiple_of(b * CAP, CAP))
+                return carry
+            lax.fori_loop(0, nb, block, 0)
+
+            def expert(l, carry):
+                xg, cg = xg_ref[l], cg_ref[l]
+                _, _, d_gate, d_up, scaled = expert_parts(xg, cg, sg_ref[l], wg[l], wu[l], wd[l])
+                ag[l] += dot(xg, d_gate, ((0,), (0,)))
+                au[l] += dot(xg, d_up, ((0,), (0,)))
+                ad[l] += dot(scaled, cg, ((0,), (0,)))
+                return carry
+            lax.fori_loop(0, local, expert, 0)
+
+            @pl.when(q == 0)
+            def _():
+                between()
+            return carry
+        lax.fori_loop(0, chunks, chunk, 0)
+
+    begin(1)
+    weights = [pltpu.make_async_copy(a, b, wsem.at[i]) for i, (a, b) in enumerate(((wg_hbm, wg), (wu_hbm, wu), (wd_hbm, wd)))]
+    for copy in weights:
+        copy.start()
+    ag[...] = jnp.zeros_like(ag)
+    au[...] = jnp.zeros_like(au)
+    ad[...] = jnp.zeros_like(ad)
+    for copy in weights:
+        copy.wait()
+
+    def next_of(j):
+        def between():
+            @pl.when(j + 1 < reps)
+            def _():
+                forward(j + 1)
+
+            @pl.when(j + 2 < reps)
+            def _():
+                begin(j + 2)
+        return between
+
+    replica(xown_hbm, cown_hbm, gown_ref, next_of(0))
+    end(1)
+
+    def others(j, carry):
+        replica(xoth_hbm.at[j - 1], coth_hbm.at[j - 1], goth.at[j - 1], next_of(j))
+
+        @pl.when(j + 1 < reps)
+        def _():
+            end(j + 1)
+        return carry
+    lax.fori_loop(1, reps, others, 0)
+    outs = [pltpu.make_async_copy(a, b, wsem.at[i]) for i, (a, b) in enumerate(((ag, og_hbm), (au, ou_hbm), (ad, od_hbm)))]
+    for copy in outs:
+        copy.start()
+    for copy in outs:
+        copy.wait()
+
+
+def moe_spread_sums(xown, cown, xcol, ccol, gown, gcol, wg, wu, wd, nb=4):
+    shards, count, width = xown.shape
+    reps = xcol.shape[0]
+    local, _, hidden = wg.shape
+    any_ = pl.BlockSpec(memory_space=pl.ANY)
+    v = pl.BlockSpec(memory_space=pltpu.VMEM)
+    rows = nb * CAP
+    n = PlaneGather.copies(shards)
+    slots = reps * shards * local * CAP
+    outs = pl.pallas_call(
+        functools.partial(spread_kernel, nb),
+        out_shape=[jax.ShapeDtypeStruct((reps - 1, shards, count, width), bf16)] * 2
+        + [jax.ShapeDtypeStruct(w.shape, f32) for w in (wg, wu, wd)],
+        in_specs=[any_, any_, any_, any_, v, v, any_, any_, any_],
+        out_specs=[any_] * 5,
+        scratch_shapes=[
+            pltpu.VMEM((2, nb, count, width), bf16), pltpu.VMEM((2, nb, count, width), bf16),
+            pltpu.VMEM(wg.shape, bf16), pltpu.VMEM(wu.shape, bf16), pltpu.VMEM(wd.shape, bf16),
+            pltpu.VMEM(wg.shape, f32), pltpu.VMEM(wu.shape, f32), pltpu.VMEM(wd.shape, f32),
+            pltpu.VMEM((local, rows, width), bf16), pltpu.VMEM((local, rows, width), bf16), pltpu.VMEM((local, rows, 1), f32),
+            pltpu.VMEM((reps - 1, shards, *gown.shape[1:]), f32),
+            pltpu.SemaphoreType.DMA((reps - 1, 3, n)), pltpu.SemaphoreType.DMA((reps - 1, 3, n)),
+            pltpu.SemaphoreType.DMA((2, 2)), pltpu.SemaphoreType.DMA((3,)), pltpu.SemaphoreType.DMA((2,)),
+        ],
+        compiler_params=pltpu.CompilerParams(vmem_limit_bytes=60 << 20, has_side_effects=True),
+        cost_estimate=pl.CostEstimate(
+            flops=12 * slots * width * hidden, transcendentals=slots * hidden, bytes_accessed=4 * reps * shards * count * width
+        ),
+        name="spread_expert_sums",
+    )(xown, cown, xcol, ccol, gown, gcol, wg, wu, wd)
+    return outs[2:]
 
 def rotary_tables(count):
     half = HEAD_SIZE // 2
@@ -355,45 +788,6 @@
     first, second = shaped[..., :half], shaped[..., half:]
     c, s = cosine[:, None, :half], sine[:, None, :half]
     return jnp.concatenate([first * c + second * s, second * c - first * s], axis=-1).reshape(rows.shape)
-
-
-def own_part(x, c, gates, first, w_gate, w_up, w_down):
-    local, width, hidden = w_gate.shape
-    shards, count, _ = x.shape
-    mine = lax.dynamic_slice_in_dim(gates, first, local, axis=1)
-    named = mine > 0
-    place = jnp.arange(count)
-    earlier = (place[:, None] < place[None, :]).astype(bf16)
-    rank = jnp.einsum("bls,st->blt", named.astype(bf16), earlier, preferred_element_type=f32)
-    here = (rank[:, :, None, :] == jnp.arange(CAP, dtype=f32)[None, None, :, None]) & named[:, :, None, :]
-    one_hot = here.astype(bf16)
-    slot_gate = jnp.sum(jnp.where(here, mine[:, :, None, :], 0.0), axis=3)
-    xg = jnp.einsum("blst,btd->lbsd", one_hot, x).reshape(local, -1, width)
-    cg = jnp.einsum("blst,btd->lbsd", one_hot, c).reshape(local, -1, width)
-    scale = branch_scale * slot_gate.transpose(1, 0, 2).reshape(local, -1)[:, :, None]
-    gate_part = jnp.einsum("lmd,ldf->lmf", xg, w_gate, preferred_element_type=f32)
-    up_part = jnp.einsum("lmd,ldf->lmf", xg, w_up, preferred_element_type=f32)
-    raw = jnp.einsum("lmd,lfd->lmf", cg, w_down, preferred_element_type=f32)
-    sigma = jax.nn.sigmoid(gate_part)
-    act = gate_part * sigma
-    inner = act * up_part
-    d_inner = raw * scale
-    d_gate = (d_inner * up_part * sigma * (1.0 + gate_part * (1.0 - sigma))).astype(bf16)
-    d_up = (d_inner * act).astype(bf16)
-    scaled = (inner * scale).astype(bf16)
-    out_rows = jnp.einsum("lmf,lfd->lmd", scaled, w_down, preferred_element_type=f32).astype(bf16)
-    d_rows = jnp.einsum("lmf,ldf->lmd", d_gate, w_gate, preferred_element_type=f32)
-    d_rows = (d_rows + jnp.einsum("lmf,ldf->lmd", d_up, w_up, preferred_element_type=f32)).astype(bf16)
-    slot_d_gate = branch_scale * jnp.sum(inner * raw, axis=2)
-    shape4 = (local, shards, CAP, width)
-    mix = jnp.einsum("blst,lbsd->btd", one_hot, out_rows.reshape(shape4), preferred_element_type=f32)
-    d_in = jnp.einsum("blst,lbsd->btd", one_hot, d_rows.reshape(shape4), preferred_element_type=f32)
-    dg = jnp.sum(jnp.where(here, slot_d_gate.reshape(local, shards, CAP).transpose(1, 0, 2)[..., None], 0.0), axis=2)
-    dg_all = jnp.zeros((shards, count, LANES), f32)
-    dg_all = lax.dynamic_update_slice(dg_all, dg.transpose(0, 2, 1), (0, 0, first))
-    back = jnp.concatenate([mix, d_in, dg_all], axis=2).astype(bf16).reshape(shards * count, -1)
-    back = lax.psum_scatter(back, "shard", scatter_dimension=0, tiled=True).astype(f32)
-    return back[:, :width], back[:, width:2 * width], back[:, 2 * width:2 * width + gates.shape[1]].T
 
 
 def body(
@@ -409,11 +803,10 @@
     group = QUERY_HEADS // KEY_VALUE_HEADS
     spread = reps <= MOST_GATHERED
     axes = ("rep", "shard") if spread else "shard"
-    all_cot = lax.all_gather(cotangent, axes, axis=0).reshape(-1, count, width)
     cosine, sine = rotary_tables(count)
     mine = pack(w_query, key_weight, value_weight, w_out, w_router, norm_attn, norm_moe)
-    packed, query, keys, values, attended, hidden_one, normed_two, gates, normed_one = front(
-        tokens, prefix, routes.T, mine, cosine, sine, experts, kv_width
+    packed, cot_own, cot_col, query, keys, values, attended, hidden_one, normed_two, gates, normed_one = front(
+        tokens, prefix, routes.T, mine, cotangent, cosine, sine, experts, kv_width, spread
     )
     packed = packed.reshape(width, -1)
     cuts = [width, width + kv_width, width + 2 * kv_width, 2 * width + 2 * kv_width]
@@ -421,13 +814,15 @@
     wr = small[:, :experts]
     gain_one = small[:, experts].astype(f32)[None, :]
     gain_two = small[:, experts + 1].astype(f32)[None, :]
-    all_x = lax.all_gather(normed_two, axes, axis=0).reshape(-1, count, width)
-    all_gates = lax.all_gather(gates, axes, axis=0).reshape(-1, experts, count)
-    own = rep * shards if spread else 0
-    rows = lambda a: lax.dynamic_slice_in_dim(a, own, shards, axis=0)
-    mix, d_in, d_gates = own_part(rows(all_x), rows(all_cot), rows(all_gates), me * local, w_gate, w_up, w_down)
-    sums = moe_sums(all_x, all_cot, all_gates, w_gate, w_up, w_down)
-    if not spread:
+    x_own, x_col, gates_own, gates_col, back, d_gates = moe_own(
+        normed_two, gates, cot_own, w_gate, w_up, w_down, spread
+    )
+    mix, d_in = back[:, :width], back[:, width:]
+    d_gates = d_gates.reshape(experts, count)
+    if spread:
+        sums = moe_spread_sums(x_own, cot_own, x_col, cot_col, gates_own, gates_col, w_gate, w_up, w_down)
+    else:
+        sums = moe_sums(x_own, cot_own, gates_own, w_gate, w_up, w_down)
         sums = [lax.psum(a.astype(bf16), "rep").astype(f32) for a in sums]
     d_w_gate, d_w_up, d_w_down = sums
 

time: 803 us -> 610 us (0.76)
  waiting for transfers between devices: 385 us -> 63.2 us
  Pallas kernels: 201 us -> 433 us
  matrix products: 132 us -> 40.5 us
    all_gather x3 -> x0, waiting for transfers between devices: 263 us -> none  [the longest x1 116 us: body(): all_x = lax.all_gather(normed_two, axes, axis=0).reshape(-1, count, width)]
    pallas_call x2 -> x3, Pallas kernels: 201 us -> 433 us  [the longest x1 269 us: moe_spread_sums(): pl.pallas_call(functools.partial(spread_kernel, nb), out_shape=[jax.Shape...]
    dot_general x11 -> x0, matrix products: 89.8 us -> none  [the longest x1 14.1 us: own_part(): jnp.einsum('lmf,ldf->lmd', d_gate, w_gate, preferred_element_type=f32)]
    reduce_scatter x1 -> x0, waiting for transfers between devices: 57.7 us -> none  [own_part(): lax.psum_scatter(back, 'shard', scatter_dimension=0, tiled=True).astype(f32)]
    concatenate x2 -> x0, local copies, waits for them, and re-layouts: 12.9 us -> none  [own_part(): jnp.concatenate([mix, d_in, dg_all], axis=2).astype(bf16)]
    unnamed x40 -> x70, local copies, waits for them, and re-layouts: 10.2 us -> 22.4 us
  transfers between devices with their start and end apart: 6 -> 2, of which waited for: 5 -> 1; matrix products, arithmetic and copies ran while one was open for 5% -> 0% of each run, Pallas kernels for 18% -> 45%
where the time goes in v3:
time: 610 us; the launch traced here: 603 us
  Pallas kernels  433 us (71%)
  waiting for transfers between devices  63.2 us (10%)
  matrix products  40.5 us (7%)
  local copies, waits for them, and re-layouts  34.8 us (6%)
  other arithmetic  16.1 us (3%)
  between operations  15.6 us (3%)
    pallas_call x1, Pallas kernels, moe_spread_sums(): pl.pallas_call(functools.partial(spread_kernel, nb), out_shape=[jax.Shape...  269 us
    pallas_call x1, Pallas kernels, moe_own(): pl.pallas_call(functools.partial(own_kernel, spread, nb), out_shape=[sds(...  95.5 us
    pallas_call x1, Pallas kernels, front(): pl.pallas_call(functools.partial(front_kernel, spread), out_shape=[sds((s...  68.1 us
    reduce_scatter x1, waiting for transfers between devices, body(): shares = lax.psum_scatter(shares, 'shard', scatter_dimension=0, tiled=True)  63.1 us
    unnamed x70, local copies, waits for them, and re-layouts  22.4 us
    dot_general x6, matrix products, dot(): lax.dot_general(left, right, (contract, ((), ())), preferred_element_type...  15.1 us
  transfers between devices with their start and end apart: 2, of which 1 were waited for; matrix products, arithmetic and copies ran while one was open for 0% of the time, Pallas kernels for 45%

profile of v3, /device:TPU:0, one launch (start us, length us, event | category | flops | bytes accessed | tf_op | source)
XLA Modules:
  0.0 603.2 jit_solution(15155290037347997722)
XLA Ops:
  7.2 0.2 fusion.41
  7.5 0.8 copy.67.sin_ref
  8.3 0.8 copy.66.cos_ref
  9.7 1.8 fusion.30
  11.5 0.7 pad_maximum_fusion.6
  12.3 0.7 fusion.40
  13.1 1.0 constant_dynamic-update-slice_fusion.3
  14.0 0.9 constant_dynamic-update-slice_fusion.2
  15.0 0.9 constant_dynamic-update-slice_fusion.1
  15.9 1.0 constant_dynamic-update-slice_fusion
  16.9 0.9 copy-done.7
  17.8 68.1 %front.1 = (bf16[8,128,3200]{2,1,0:T(8,128)(2,1)}, bf16[8,256,1024]{2,1,0:T(8,128)(2,1)}, bf16[4,256,1024]{2,1,0:T(8,128)(2,1)}, bf16[256,1024]{1,0:T(8,128)(2,1...) custom-call(s32[1]{0:T(128)} %copy.100.prefix_ref, ...), custom_call_target="tpu_custom_call" | custom-call | tf_op jit(solution)/shard_map/front/pallas_call | solution.py:353
  85.9 1.8 copy.68
  87.7 1.4 multiply_reduce_fusion.2
  89.0 0.6 multiply_multiply_fusion.1
  89.6 1.1 copy.70
  90.7 2.0 copy.69
  92.8 1.2 slice_convert_fusion
  94.2 95.5 %own_experts.1 = (bf16[8,256,1024]{2,1,0:T(8,128)(2,1)}, bf16[4,256,1024]{2,1,0:T(8,128)(2,1)}, f32[8,32,256]{2,1,0:T(8,128)}, f32[4,32,256]{2,1,0:T(8,128)}, f32[256,2048]{1,0:T(8,128)}, /*index=5*/f32[8,4,256]{2,1,0:T(4,128)}) custom-call(bf16[256,1024]{1,0:T(8,128)(2,1)} %get-tuple-element.33.x_ref, f32[32,256]{1,0:T(8,128)} %get-tuple-element.34.gates_ref, ...), custom_call_target="tpu_custom_call" | custom-call | tf_op jit(solution)/shard_map/own_experts/pallas_call | solution.py:587
  189.7 0.8 reshape.142
  190.8 2.6 multiply_reduce_fusion
  193.4 1.9 convert_add_fusion
  195.3 2.4 fusion.20
  197.7 0.2 copy.72
  197.9 2.8 fusion.56
  200.7 3.5 fusion.55
  204.2 3.0 fusion.27
  207.2 8.0 %fusion.23 = f32[256,8,64]{0,2,1:T(8,128)} fusion(bf16[256,8,2,64]{0,3,2,1:T(8,128)(2,1)S(1)} %bitcast.106, f32[8,256,256,2]{2,1,3,0:T(8,128)} %fusion.56, f32[8,2,256,256]{2,3,1,0:T(8,128)} %get-tuple-element.114, f32[8,2,256]{2,1,0:T(2,128)S(1)} %get-tuple-element.113), kind=kOutput, calls=%fused_computation.34 | convolution fusion | flops 141562112 | bytes 9453568 | tf_op jit(solution)/shard_map/ngts,tngd->snd/dot_general | solution.py:854
  215.2 8.2 %fusion.19 = f32[8,64,2,256]{3,1,2,0:T(8,128)} fusion(bf16[256,8,64,1]{0,2,3,1:T(8,128)(2,1)S(1)} %bitcast.108, f32[8,256,256,2]{2,1,3,0:T(8,128)} %fusion.56, f32[8,2,256,256]{2,3,1,0:T(8,128)} %get-tuple-element.114, f32[8,2,256]{2,1,0:T(2,128)S(1)} %get-tuple-element.113), kind=kOutput, calls=%fused_computation.27 | convolution fusion | flops 141562112 | bytes 9715712 | tf_op jit(solution)/shard_map/ngts,snd->tngd/dot_general | solution.py:853
  223.3 0.6 multiply_multiply_fusion
  224.1 1.9 convolution_convert_fusion.1
  226.0 1.1 add_convert_fusion.2
  227.4 5.4 fusion.36
  233.1 2.7 convolution_convert_fusion
  235.8 3.1 fusion.3
  238.9 63.1 %reduce-scatter.2.cloned.1.call-done = bf16[128,3200]{1,0:T(8,128)(2,1)} async-done(((bf16[1024,3200]{1,0:T(8,128)(2,1)}), bf16[128,3200]{1,0:T(8,128)(2,1)}) %reduce-scatter.2.cloned.1.call-update) | async-done | bytes 819216 | tf_op jit(solution)/shard_map/reduce_scatter | solution.py:866
  302.2 269.3 %spread_expert_sums.1 = (bf16[3,8,256,1024]{3,2,1,0:T(8,128)(2,1)}, bf16[3,8,256,1024]{3,2,1,0:T(8,128)(2,1)}, f32[4,1024,512]{2,1,0:T(8,128)}, f32[4,1024,512]{2,1,0:T(8,128)}, f32[4,512,1024]{2,1,0:T(8,128)}) custom-call(bf16[8,256,1024]{2,1,0:T(8,128)(2,1)} %get-tuple-element.44.xown_hbm, bf16[8,256,1024]{2,1,0:T(8,128)(2,1)} %get-tuple-element.35.c_hbm.cown_hbm, ...), custom_call_target="tpu_custom_call" | custom-call | flops 77309411328 | bytes 33554432 | tf_op jit(solution)/shard_map/spread_expert_sums/pallas_call | solution.py:740
  571.5 1.3 fusion.33
  572.8 0.8 slice.98
  573.6 0.7 copy.79
  574.3 1.3 convert_element_type.86
  575.6 0.7 slice_reduce_fusion
  576.3 2.0 fusion.54
  578.2 1.1 fusion.53
  579.3 8.0 %copy.101 = f32[4,1024,512]{2,1,0:T(8,128)} copy(f32[4,1024,512]{2,1,0:T(8,128)} %get-tuple-element.137) | data formatting | bytes 16777216
  587.3 4.3 copy.102
  591.6 1.0 slice-done.1
  592.5 3.4 copy.103
  (87 shorter events, 1.5 us)
Async XLA Ops:
  7.2 294.9 %reduce-scatter.2.cloned.1.call-start = ((), (), s32[]{:S(2)}) async-start(), calls=%async_computation.1 | async-start | bytes 7372800 | tf_op jit(solution)/shard_map/reduce_scatter | solution.py:866
  16.9 0.9 copy-start.7
  89.6 101.2 %copy-start.19 = (f32[256]{0:T(256)}, f32[256]{0:T(256)S(1)}, u32[]{:S(2)}) copy-start(f32[256]{0:T(256)S(1)} %get-tuple-element.109) | copy-start | bytes 3076
  94.2 96.6 %copy-start.16 = (f32[1024,1]{0,1:T(1,128)}, f32[1024,1]{0,1:T(1,128)S(1)}, u32[]{:S(2)}) copy-start(f32[1024,1]{0,1:T(1,128)S(1)} %copy.90) | copy-start | bytes 12292
  94.2 96.3 %copy-start.12 = (f32[32,256]{1,0:T(8,128)S(1)}, f32[32,256]{1,0:T(8,128)}, u32[]{:S(2)}) copy-start(f32[32,256]{1,0:T(8,128)} %get-tuple-element.34.gates_ref) | copy-start | bytes 98308
  94.2 96.4 %copy-start.4 = (bf16[256,1024]{1,0:T(8,128)(2,1)S(1)}, bf16[256,1024]{1,0:T(8,128)(2,1)}, u32[]{:S(2)}) copy-start(bf16[256,1024]{1,0:T(8,128)(2,1)} %get-tuple-element.33.x_ref) | copy-start | bytes 1572868
  94.2 96.6 %copy-start = (f32[256,1024]{1,0:T(8,128)S(1)}, f32[256,1024]{1,0:T(8,128)}, u32[]{:S(2)}) copy-start(f32[256,1024]{1,0:T(8,128)} %get-tuple-element.32) | copy-start | bytes 3145732
  189.7 3.7 copy-start.3
  190.5 2.9 copy-start.5
  195.3 5.4 copy-start.11
  197.9 2.8 copy-start.13
  197.9 2.8 copy-start.15
  207.1 20.2 %copy-start.14 = (bf16[8,64,256]{2,1,0:T(8,128)(2,1)}, bf16[8,64,256]{2,1,0:T(8,128)(2,1)S(1)}, u32[]{:S(2)}) copy-start(bf16[8,64,256]{2,1,0:T(8,128)(2,1)S(1)} %fusion.27) | copy-start | bytes 786436
  215.2 8.2 %copy-start.21 = (f32[256]{0:T(256)S(1)}, f32[256]{0:T(256)}, u32[]{:S(2)}) copy-start(f32[256]{0:T(256)} %fusion.30) | copy-start | bytes 3076
  215.2 8.9 %copy-start.20 = (bf16[1024]{0:T(1024)(128)(2,1)S(1)}, bf16[1024]{0:T(1024)(128)(2,1)}, u32[]{:S(2)}) copy-start(bf16[1024]{0:T(1024)(128)(2,1)} %get-tuple-element.88) | copy-start | bytes 6148
  223.9 8.9 %copy-start.23 = (f32[256]{0:T(256)}, f32[256]{0:T(256)S(1)}, u32[]{:S(2)}) copy-start(f32[256]{0:T(256)S(1)} %get-tuple-element.107) | copy-start | bytes 3076
  224.1 8.7 %copy-start.17 = (f32[1024,1]{0,1:T(1,128)}, f32[1024,1]{0,1:T(1,128)S(1)}, u32[]{:S(2)}) copy-start(f32[1024,1]{0,1:T(1,128)S(1)} %copy.91) | copy-start | bytes 12292
  224.1 3.0 copy-start.9
  227.3 5.5 copy-start.10
  227.4 5.5 copy-start.6
  238.9 333.9 %all-reduce.4.cloned.1.call-start = ((), (), s32[]{:S(2)}) async-start(), calls=%async_computation.2 | async-start | bytes 1638400 | tf_op jit(solution)/shard_map/psum | solution.py:867
  302.1 269.3 %copy-start.25 = (f32[256]{0:T(256)S(1)}, f32[256]{0:T(256)}, u32[]{:S(2)}) copy-start(f32[256]{0:T(256)} %get-tuple-element.93) | copy-start | bytes 3076
  302.1 269.4 %copy-start.2 = (bf16[256,1024]{1,0:T(8,128)(2,1)S(1)}, bf16[256,1024]{1,0:T(8,128)(2,1)}, u32[]{:S(2)}) copy-start(bf16[256,1024]{1,0:T(8,128)(2,1)} %tok_ref.1) | copy-start | bytes 1572868
  302.1 269.3 %copy-start.8 = (f32[256,1024]{1,0:T(8,128)S(1)}, f32[256,1024]{1,0:T(8,128)}, u32[]{:S(2)}) copy-start(f32[256,1024]{1,0:T(8,128)} %get-tuple-element.115) | copy-start | bytes 3145732
  302.1 269.3 %copy-start.18 = (f32[1024,1]{0,1:T(1,128)S(1)}, f32[1024,1]{0,1:T(1,128)}, u32[]{:S(2)}) copy-start(f32[1024,1]{0,1:T(1,128)} %copy-done.17) | copy-start | bytes 12292
  302.1 269.3 %copy-start.22 = (f32[256]{0:T(256)S(1)}, f32[256]{0:T(256)}, u32[]{:S(2)}) copy-start(f32[256]{0:T(256)} %get-tuple-element.106) | copy-start | bytes 3076
  302.2 269.3 %copy-start.24 = (f32[256]{0:T(256)S(1)}, f32[256]{0:T(256)}, u32[]{:S(2)}) copy-start(f32[256]{0:T(256)} %copy-done.23) | copy-start | bytes 3076
  572.8 5.4 copy-start.1
  576.3 11.0 %slice-start.2 = ((s8[8388608]{0:T(1024)(128)(4,1)}), s8[4194304]{0:T(1024)(128)(4,1)S(1)}, s32[]{:S(2)}) async-start(s8[8388608]{0:T(1024)(128)(4,1)} %bitcast.91), calls=%async_computation.5 | async-start | bytes 8388608
  579.3 8.0 %slice-start.3 = ((s8[8388608]{0:T(1024)(128)(4,1)}), s8[4194304]{0:T(1024)(128)(4,1)S(1)}, s32[]{:S(2)}) async-start(s8[8388608]{0:T(1024)(128)(4,1)} %bitcast.91), calls=%async_computation.6 | async-start | bytes 8388608
  579.3 12.2 %slice-start = ((s8[8388608]{0:T(1024)(128)(4,1)}), s8[4194304]{0:T(1024)(128)(4,1)S(1)}, s32[]{:S(2)}) async-start(s8[8388608]{0:T(1024)(128)(4,1)} %bitcast.89), calls=%async_computation.3 | async-start | bytes 8388608
  587.3 5.2 slice-start.1
Sparse Core Ops, SparseCore 0:
  239.0 63.0 reduce-scatter.1
  304.6 44.6 all-reduce.3
